TPU v7x, 32 devices: a whole 2x2x4 slice. The times are simulated.
32 devices in a mesh: fsdp: 16 (over z, x, core), rep: 2 (over y).
Axes of the slice: x: 2, y: 2, z: 4, core: 2. Of those that a mesh axis runs over, the one named last changes fastest.
Arguments:
- tokens: bfloat16 [32768, 768], P(('fsdp', 'rep')), may hold values from -6 to 6
- w_qkv: bfloat16 [1769472], P('fsdp'), may hold values from -0.21875 to 0.21875
- w_out: bfloat16 [589824], P('fsdp'), may hold values from -0.875 to 0.875
- w_fc1: bfloat16 [2359296], P('fsdp'), may hold values from -0.21875 to 0.21875
- w_fc2: bfloat16 [2359296], P('fsdp'), may hold values from -0.109375 to 0.109375
- gains: bfloat16 [1536], P('fsdp'), may hold values from 0.099609375 to 1.8984375
- biases: bfloat16 [7680], P('fsdp'), may hold values from -3 to 3
- segment: int32 [32768], P(('fsdp', 'rep')), may hold values from 0 to 40, as said below
- cotangent: bfloat16 [32768, 768], P(('fsdp', 'rep')), may hold values from -6 to 6
Outputs:
- output: bfloat16 [32768, 768], P(('fsdp', 'rep'))
- grad_tokens: float32 [32768, 768], P(('fsdp', 'rep'))
- grad_qkv: float32 [1769472], P('fsdp')
- grad_out: float32 [589824], P('fsdp')
- grad_fc1: float32 [2359296], P('fsdp')
- grad_fc2: float32 [2359296], P('fsdp')
- grad_gains: float32 [1536], P('fsdp')
- grad_biases: float32 [7680], P('fsdp')
Inputs may be any that keep to these rules, and one draw needn't show every extreme that they name: Within the 1024 tokens of one device, segment numbers start at 0, never fall and rise by at most one from token to token, so every image lies whole on one device. Every image but the last of a device has 25, 64 or 900 tokens; the last image of each device may be cut short by the device's end to as few as 1 token and is still a segment of its own. Some device holds an image of exactly 900 tokens, and some device holds only images of 25 tokens apart from its cut last one.
All inputs are finite; a program needn't handle non-finite values.
Results may differ from a plain program's by a relative error of at most 0.013.
Values may be sent and summed in bfloat16 or wider, within the bound.
No kernel may reach another device: no remote copies, remote signals or barrier semaphores. Data moves between devices by JAX's collectives and lax.ppermute only.
A program may use at most 192 MiB of HBM per device.

v0:
```python
import jax
import jax.numpy as jnp
from jax import lax
from jax.sharding import PartitionSpec as P

D = 768
H = 12
HD = 64
FF = 3072


epsilon_norm = 1e-06
score_scale = 0.125
masked_low = -1e30


def normalize(values, gain, shift):
    center = values - jnp.mean(values, axis=-1, keepdims=True)
    spread = jnp.mean(center * center, axis=-1, keepdims=True)
    return center * lax.rsqrt(spread + epsilon_norm) * gain + shift


def gelu_exact(values):
    return jax.nn.gelu(values, approximate=False)


def unpack(gains, biases):
    return (
        gains[:D],
        gains[D:],
        biases[:D],
        biases[D : 2 * D],
        biases[2 * D : 3 * D],
        biases[3 * D : 4 * D],
        biases[4 * D : 5 * D],
        biases[5 * D : 5 * D + FF],
        biases[5 * D + FF :],
    )


def shape_weights(gathered):
    return (
        gathered[0].reshape(D, 3 * D),
        gathered[1].reshape(D, D),
        gathered[2].reshape(D, FF),
        gathered[3].reshape(FF, D),
    )


def contract_last(left, right):
    return lax.dot_general(
        left, right, (((1,), (1,)), ((), ())), preferred_element_type=jnp.float32
    )


def contract_first(left, right):
    return lax.dot_general(
        left, right, (((0,), (0,)), ((), ())), preferred_element_type=jnp.float32
    )


def split_heads(matrix):
    return matrix.reshape(matrix.shape[0], H, HD).transpose(1, 0, 2)


def merge_heads(stacked):
    return stacked.transpose(1, 0, 2).reshape(stacked.shape[1], H * HD)


def column_sum(matrix):
    return jnp.sum(matrix.astype(jnp.float32), axis=0)


def shards(tokens, w_qkv, w_out, w_fc1, w_fc2, gains, biases, segment, cotangent):
    row_count = tokens.shape[0]
    block_rows = min(512, row_count)
    block_count = row_count // block_rows
    segment_blocks = segment.reshape(block_count, block_rows)
    gathered = (
        lax.all_gather(w_qkv, "fsdp", axis=0, tiled=True),
        lax.all_gather(w_out, "fsdp", axis=0, tiled=True),
        lax.all_gather(w_fc1, "fsdp", axis=0, tiled=True),
        lax.all_gather(w_fc2, "fsdp", axis=0, tiled=True),
        lax.all_gather(gains, "fsdp", axis=0, tiled=True),
        lax.all_gather(biases, "fsdp", axis=0, tiled=True),
    )
    weight_qkv, weight_out, weight_up, weight_down = shape_weights(gathered)
    (
        gain_one,
        gain_two,
        shift_one,
        bias_query,
        bias_value,
        bias_out,
        shift_two,
        bias_up,
        bias_down,
    ) = unpack(gathered[4].astype(jnp.float32), gathered[5].astype(jnp.float32))
    tokens_f = tokens.astype(jnp.float32)
    normed = normalize(tokens_f, gain_one, shift_one).astype(jnp.bfloat16)
    projected = jnp.dot(normed, weight_qkv, preferred_element_type=jnp.float32)
    queries = (projected[:, :D] + bias_query).astype(jnp.bfloat16)
    keys_all = projected[:, D : 2 * D].astype(jnp.bfloat16)
    values_all = (projected[:, 2 * D :] + bias_value).astype(jnp.bfloat16)
    query_heads = split_heads(queries)
    key_heads = split_heads(keys_all)
    value_heads = split_heads(values_all)

    def head_forward(head_in):
        query_h, key_h, value_h = head_in

        def one_block(block_in):
            query_b, segment_b = block_in
            scores = contract_last(query_b, key_h) * score_scale
            scores = jnp.where(segment_b[:, None] == segment[None, :], scores, masked_low)
            row_max = jnp.max(scores, axis=-1, keepdims=True)
            exponent = jnp.exp(scores - row_max)
            total_sum = jnp.sum(exponent, axis=-1, keepdims=True)
            probs = (exponent / total_sum).astype(jnp.bfloat16)
            return (
                jnp.dot(probs, value_h, preferred_element_type=jnp.float32),
                (row_max + jnp.log(total_sum))[:, 0],
            )

        out_blocks, log_blocks = lax.map(
            one_block, (query_h.reshape(block_count, block_rows, HD), segment_blocks)
        )
        return (out_blocks.reshape(row_count, HD), log_blocks.reshape(row_count))

    attended_heads, log_totals = lax.map(head_forward, (query_heads, key_heads, value_heads))
    attended = merge_heads(attended_heads).astype(jnp.bfloat16)
    middle = tokens_f + jnp.dot(attended, weight_out, preferred_element_type=jnp.float32) + bias_out
    normed_two = normalize(middle, gain_two, shift_two).astype(jnp.bfloat16)
    hidden_pre = jnp.dot(normed_two, weight_up, preferred_element_type=jnp.float32) + bias_up
    activated = gelu_exact(hidden_pre).astype(jnp.bfloat16)
    output = (
        middle + jnp.dot(activated, weight_down, preferred_element_type=jnp.float32) + bias_down
    )
    again = (
        lax.all_gather(w_qkv, "fsdp", axis=0, tiled=True),
        lax.all_gather(w_out, "fsdp", axis=0, tiled=True),
        lax.all_gather(w_fc1, "fsdp", axis=0, tiled=True),
        lax.all_gather(w_fc2, "fsdp", axis=0, tiled=True),
        lax.all_gather(gains, "fsdp", axis=0, tiled=True),
        lax.all_gather(biases, "fsdp", axis=0, tiled=True),
    )
    weight_qkv, weight_out, weight_up, weight_down = shape_weights(again)
    (
        gain_one,
        gain_two,
        shift_one,
        bias_query,
        bias_value,
        bias_out,
        shift_two,
        bias_up,
        bias_down,
    ) = unpack(again[4].astype(jnp.float32), again[5].astype(jnp.float32))
    grad_down = contract_first(activated, cotangent)
    grad_bias_down = column_sum(cotangent)
    grad_act = contract_last(cotangent, weight_down)
    gelu_value, gelu_pull = jax.vjp(gelu_exact, hidden_pre)
    grad_hidden = gelu_pull(grad_act)[0].astype(jnp.bfloat16)
    grad_up = contract_first(normed_two, grad_hidden)
    grad_bias_up = column_sum(grad_hidden)
    grad_normed_two = contract_last(grad_hidden, weight_up)
    norm_two_value, norm_two_pull = jax.vjp(normalize, middle, gain_two, shift_two)
    grad_middle_norm, grad_gain_two, grad_shift_two = norm_two_pull(grad_normed_two)
    grad_middle = cotangent.astype(jnp.float32) + grad_middle_norm
    grad_branch = grad_middle.astype(jnp.bfloat16)
    grad_weight_out = contract_first(attended, grad_branch)
    grad_bias_out = column_sum(grad_branch)
    grad_attended = contract_last(grad_branch, weight_out).astype(jnp.bfloat16)
    grad_heads = split_heads(grad_attended)

    def head_backward(head_in):
        query_h, key_h, value_h, grad_h, log_h = head_in

        def step(carry, block_in):
            key_grad, value_grad = carry
            query_b, segment_b, grad_b, log_b = block_in
            scores = contract_last(query_b, key_h) * score_scale
            scores = jnp.where(segment_b[:, None] == segment[None, :], scores, masked_low)
            probs = jnp.exp(scores - log_b[:, None])
            probs_low = probs.astype(jnp.bfloat16)
            prob_grad = contract_last(grad_b, value_h)
            centre = jnp.sum(probs * prob_grad, axis=-1, keepdims=True)
            score_grad = (probs * (prob_grad - centre)).astype(jnp.bfloat16)
            query_grad = (
                jnp.dot(score_grad, key_h, preferred_element_type=jnp.float32) * score_scale
            )
            key_grad = key_grad + contract_first(score_grad, query_b) * score_scale
            value_grad = value_grad + contract_first(probs_low, grad_b)
            return ((key_grad, value_grad), query_grad)

        zero_rows = jnp.zeros((row_count, HD), jnp.float32)
        (key_grad, value_grad), query_grad = lax.scan(
            step,
            (zero_rows, zero_rows),
            (
                query_h.reshape(block_count, block_rows, HD),
                segment_blocks,
                grad_h.reshape(block_count, block_rows, HD),
                log_h.reshape(block_count, block_rows),
            ),
        )
        return (query_grad.reshape(row_count, HD), key_grad, value_grad)

    grad_query_h, grad_key_h, grad_value_h = lax.map(
        head_backward, (query_heads, key_heads, value_heads, grad_heads, log_totals)
    )
    grad_projected = jnp.concatenate(
        [merge_heads(grad_query_h), merge_heads(grad_key_h), merge_heads(grad_value_h)], axis=1
    ).astype(jnp.bfloat16)
    grad_weight_qkv = contract_first(normed, grad_projected)
    grad_bias_query = column_sum(grad_projected[:, :D])
    grad_bias_value = column_sum(grad_projected[:, 2 * D :])
    grad_normed = contract_last(grad_projected, weight_qkv)
    norm_one_value, norm_one_pull = jax.vjp(normalize, tokens_f, gain_one, shift_one)
    grad_tokens_norm, grad_gain_one, grad_shift_one = norm_one_pull(grad_normed)
    grad_tokens = grad_middle + grad_tokens_norm
    local_grads = (
        grad_weight_qkv.reshape(-1),
        grad_weight_out.reshape(-1),
        grad_up.reshape(-1),
        grad_down.reshape(-1),
        jnp.concatenate([grad_gain_one, grad_gain_two]),
        jnp.concatenate(
            [
                grad_shift_one,
                grad_bias_query,
                grad_bias_value,
                grad_bias_out,
                grad_shift_two,
                grad_bias_up,
                grad_bias_down,
            ]
        ),
    )
    owned = (
        lax.psum_scatter(local_grads[0], "fsdp", scatter_dimension=0, tiled=True),
        lax.psum_scatter(local_grads[1], "fsdp", scatter_dimension=0, tiled=True),
        lax.psum_scatter(local_grads[2], "fsdp", scatter_dimension=0, tiled=True),
        lax.psum_scatter(local_grads[3], "fsdp", scatter_dimension=0, tiled=True),
        lax.psum_scatter(local_grads[4], "fsdp", scatter_dimension=0, tiled=True),
        lax.psum_scatter(local_grads[5], "fsdp", scatter_dimension=0, tiled=True),
    )
    owned = (
        lax.psum(owned[0].astype(jnp.bfloat16), "rep").astype(jnp.float32),
        lax.psum(owned[1].astype(jnp.bfloat16), "rep").astype(jnp.float32),
        lax.psum(owned[2].astype(jnp.bfloat16), "rep").astype(jnp.float32),
        lax.psum(owned[3].astype(jnp.bfloat16), "rep").astype(jnp.float32),
        lax.psum(owned[4].astype(jnp.bfloat16), "rep").astype(jnp.float32),
        lax.psum(owned[5].astype(jnp.bfloat16), "rep").astype(jnp.float32),
    )
    return (
        output.astype(jnp.bfloat16),
        grad_tokens,
        owned[0],
        owned[1],
        owned[2],
        owned[3],
        owned[4],
        owned[5],
    )


def solution(mesh):
    placed = (
        P(("fsdp", "rep"), None),
        P("fsdp"),
        P("fsdp"),
        P("fsdp"),
        P("fsdp"),
        P("fsdp"),
        P("fsdp"),
        P(("fsdp", "rep")),
        P(("fsdp", "rep"), None),
    )
    return jax.shard_map(
        shards,
        mesh=mesh,
        in_specs=placed,
        out_specs=(
            P(("fsdp", "rep"), None),
            P(("fsdp", "rep"), None),
            P("fsdp"),
            P("fsdp"),
            P("fsdp"),
            P("fsdp"),
            P("fsdp"),
            P("fsdp"),
        ),
        check_vma=False,
    )
```

profile of v0, /device:TPU:16, one launch (start us, length us, event | category | flops | bytes accessed | tf_op | source)
XLA Modules:
  0.0 1372.2 jit_solution(9369776842039899394)
XLA Ops:
  14.4 45.5 %all-reduce.9 = (bf16[1536]{0:T(1024)(128)(2,1)S(1)}, bf16[7680]{0:T(1024)(128)(2,1)S(1)}) all-reduce(bf16[1536]{0:T(1024)(128)(2,1)S(1)} %dynamic-update-slice, bf16[7680]{0:T(1024)(128)(2,1)S(1)} %dynamic-update-slice.1), channel_id=1, replica_groups=mesh['fsdp'=16,'rep'=2] {'fsdp'}, use_global_device_ids=true, to_apply=%add | all-reduce | flops 9216 | bytes 36864
  68.7 3.4 reshape.202
  72.0 25.6 %all-gather.5.cloned.1.call-done = bf16[1769472]{0:T(1024)(128)(2,1)} async-done(((bf16[110592]{0:T(1024)(128)(2,1)}), bf16[1769472]{0:T(1024)(128)(2,1)}) %all-gather.5.cloned.1.call-update) | async-done | bytes 3538960 | tf_op jit(solution)/shard_map/all_gather | solution.py:80
  97.7 7.6 reshape.197
  105.3 6.4 fusion.51
  111.8 2.3 fusion.40
  115.9 2.7 copy.65
  120.3 2.8 copy.67
  123.8 2.8 copy.66
  128.0 95.1 %while.54 = (s32[]{:T(128)}, bf16[12,1024,64]{1,2,0:T(8,128)(2,1)}, f32[12,1024]{1,0:T(8,128)}, bf16[12,1024,64]{2,1,0:T(8,128)(2,1)}, bf16[12,1024,64]{2,1,0:T(...) while((s32[]{:T(128)}, bf16[12,1024,64]{1,2,0:T(8,128)(2,1)}, ...), condition=%wide.region_7.8_spmd, body=%wide.region_2.7_spmd.sunk | while | flops 138935808 | bytes 8698710 | solution.py:130
  130.2 3.4 while.57
  138.1 3.4 while.57
  146.0 3.4 while.57
  153.9 3.4 while.57
  161.9 3.4 while.57
  169.8 3.4 while.57
  177.7 3.4 while.57
  185.6 3.4 while.57
  193.5 3.4 while.57
  201.4 3.4 while.57
  209.3 3.4 while.57
  217.2 3.4 while.57
  223.0 3.8 fusion.61
  227.3 8.5 reshape.203
  235.8 37.7 %multiply_convert_fusion.1 = (bf16[1024,3072]{1,0:T(8,128)(2,1)}, f32[1024,3072]{1,0:T(8,128)}, f32[1024,3072]{1,0:T(8,128)}) fusion(f32[3072]{0:T(1024)S(1)} %slice.63, bf16[768,3072]{1,0:T(8,128)(2,1)} %reshape.203, f32[1024,768]{0,1:T(8,128)S(1)} %get-tuple-element.449, f32[768]{0:T(1024)S(1)} %get-tuple-element.439, f32[768]{0:T(1024)S(1)} %get-tuple-element.444, ...), kind=kOutput, calls=%fused_computation.52 | convolution fusion | flops 5043388416 | bytes 39348224 | tf_op jit(solution)/shard_map/dot_general | solution.py:134
  273.5 9.6 reshape.204
  283.1 18.9 %convert_reduce_fusion = (f32[3072]{0:T(1024)}, bf16[1024,3072]{1,0:T(8,128)(2,1)}) fusion(f32[1024,3072]{1,0:T(8,128)} %get-tuple-element.425, bf16[1024,768]{1,0:T(8,128)(2,1)} %param.25, bf16[3072,768]{1,0:T(8,128)(2,1)} %reshape.204, f32[1024,3072]{1,0:T(8,128)} %get-tuple-element.450, f32[3072]{0:T(1024)S(1)} %slice.63), kind=kOutput, calls=%fused_computation.50 | convolution fusion | flops 4885312512 | bytes 37773312 | tf_op jit(solution)/shard_map/dot_general | solution.py:51
  302.0 10.5 fusion.63
  312.5 7.8 convolution_bitcast_fusion.1
  320.3 3.7 copy.71
  323.9 3.5 multiply_reduce_fusion.1
  332.2 2.8 fusion.64
  335.0 2.7 copy.72
  341.8 307.9 %while.56 = (s32[]{:T(128)}, bf16[12,1024,64]{1,2,0:T(8,128)(2,1)}, bf16[12,1024,64]{1,2,0:T(8,128)(2,1)}, bf16[12,1024,64]{1,2,0:T(8,128)(2,1)}, bf16[12,1024,6...) while((s32[]{:T(128)}, bf16[12,1024,64]{1,2,0:T(8,128)(2,1)}, ...), condition=%wide.region_16.17_spmd, body=%wide.region_12.16_spmd.sunk | while | flops 341147136 | bytes 21011884 | solution.py:209
  348.6 16.1 %while.58 = (s32[]{:T(128)}, f32[1024,64]{0,1:T(8,128)}, f32[1024,64]{0,1:T(8,128)}, bf16[2,512,64]{1,2,0:T(8,128)(2,1)S(1)}, s32[2,512]{1,0:T(2,128)S(1)}, /*in...) while((s32[]{:T(128)}, f32[1024,64]{0,1:T(8,128)}, ...), condition=%wide.region_15.15_spmd.clone, body=%wide.region_13.14_spmd.clone.sunk | while | flops 341147136 | bytes 18110612 | solution.py:197
  360.1 2.1 fusion.118
  374.3 16.1 %while.58 = (s32[]{:T(128)}, f32[1024,64]{0,1:T(8,128)}, f32[1024,64]{0,1:T(8,128)}, bf16[2,512,64]{1,2,0:T(8,128)(2,1)S(1)}, s32[2,512]{1,0:T(2,128)S(1)}, /*in...) while((s32[]{:T(128)}, f32[1024,64]{0,1:T(8,128)}, ...), condition=%wide.region_15.15_spmd.clone, body=%wide.region_13.14_spmd.clone.sunk | while | flops 341147136 | bytes 18110612 | solution.py:197
  385.7 2.1 fusion.118
  399.9 16.1 %while.58 = (s32[]{:T(128)}, f32[1024,64]{0,1:T(8,128)}, f32[1024,64]{0,1:T(8,128)}, bf16[2,512,64]{1,2,0:T(8,128)(2,1)S(1)}, s32[2,512]{1,0:T(2,128)S(1)}, /*in...) while((s32[]{:T(128)}, f32[1024,64]{0,1:T(8,128)}, ...), condition=%wide.region_15.15_spmd.clone, body=%wide.region_13.14_spmd.clone.sunk | while | flops 341147136 | bytes 18110612 | solution.py:197
  425.6 16.1 %while.58 = (s32[]{:T(128)}, f32[1024,64]{0,1:T(8,128)}, f32[1024,64]{0,1:T(8,128)}, bf16[2,512,64]{1,2,0:T(8,128)(2,1)S(1)}, s32[2,512]{1,0:T(2,128)S(1)}, /*in...) while((s32[]{:T(128)}, f32[1024,64]{0,1:T(8,128)}, ...), condition=%wide.region_15.15_spmd.clone, body=%wide.region_13.14_spmd.clone.sunk | while | flops 341147136 | bytes 18110612 | solution.py:197
  451.2 16.1 %while.58 = (s32[]{:T(128)}, f32[1024,64]{0,1:T(8,128)}, f32[1024,64]{0,1:T(8,128)}, bf16[2,512,64]{1,2,0:T(8,128)(2,1)S(1)}, s32[2,512]{1,0:T(2,128)S(1)}, /*in...) while((s32[]{:T(128)}, f32[1024,64]{0,1:T(8,128)}, ...), condition=%wide.region_15.15_spmd.clone, body=%wide.region_13.14_spmd.clone.sunk | while | flops 341147136 | bytes 18110612 | solution.py:197
  476.9 16.1 %while.58 = (s32[]{:T(128)}, f32[1024,64]{0,1:T(8,128)}, f32[1024,64]{0,1:T(8,128)}, bf16[2,512,64]{1,2,0:T(8,128)(2,1)S(1)}, s32[2,512]{1,0:T(2,128)S(1)}, /*in...) while((s32[]{:T(128)}, f32[1024,64]{0,1:T(8,128)}, ...), condition=%wide.region_15.15_spmd.clone, body=%wide.region_13.14_spmd.clone.sunk | while | flops 341147136 | bytes 18110612 | solution.py:197
  502.5 16.1 %while.58 = (s32[]{:T(128)}, f32[1024,64]{0,1:T(8,128)}, f32[1024,64]{0,1:T(8,128)}, bf16[2,512,64]{1,2,0:T(8,128)(2,1)S(1)}, s32[2,512]{1,0:T(2,128)S(1)}, /*in...) while((s32[]{:T(128)}, f32[1024,64]{0,1:T(8,128)}, ...), condition=%wide.region_15.15_spmd.clone, body=%wide.region_13.14_spmd.clone.sunk | while | flops 341147136 | bytes 18110612 | solution.py:197
  528.1 16.1 %while.58 = (s32[]{:T(128)}, f32[1024,64]{0,1:T(8,128)}, f32[1024,64]{0,1:T(8,128)}, bf16[2,512,64]{1,2,0:T(8,128)(2,1)S(1)}, s32[2,512]{1,0:T(2,128)S(1)}, /*in...) while((s32[]{:T(128)}, f32[1024,64]{0,1:T(8,128)}, ...), condition=%wide.region_15.15_spmd.clone, body=%wide.region_13.14_spmd.clone.sunk | while | flops 341147136 | bytes 18110612 | solution.py:197
  553.8 16.1 %while.58 = (s32[]{:T(128)}, f32[1024,64]{0,1:T(8,128)}, f32[1024,64]{0,1:T(8,128)}, bf16[2,512,64]{1,2,0:T(8,128)(2,1)S(1)}, s32[2,512]{1,0:T(2,128)S(1)}, /*in...) while((s32[]{:T(128)}, f32[1024,64]{0,1:T(8,128)}, ...), condition=%wide.region_15.15_spmd.clone, body=%wide.region_13.14_spmd.clone.sunk | while | flops 341147136 | bytes 18110612 | solution.py:197
  565.2 2.1 fusion.118
  579.4 16.1 %while.58 = (s32[]{:T(128)}, f32[1024,64]{0,1:T(8,128)}, f32[1024,64]{0,1:T(8,128)}, bf16[2,512,64]{1,2,0:T(8,128)(2,1)S(1)}, s32[2,512]{1,0:T(2,128)S(1)}, /*in...) while((s32[]{:T(128)}, f32[1024,64]{0,1:T(8,128)}, ...), condition=%wide.region_15.15_spmd.clone, body=%wide.region_13.14_spmd.clone.sunk | while | flops 341147136 | bytes 18110612 | solution.py:197
  605.1 16.1 %while.58 = (s32[]{:T(128)}, f32[1024,64]{0,1:T(8,128)}, f32[1024,64]{0,1:T(8,128)}, bf16[2,512,64]{1,2,0:T(8,128)(2,1)S(1)}, s32[2,512]{1,0:T(2,128)S(1)}, /*in...) while((s32[]{:T(128)}, f32[1024,64]{0,1:T(8,128)}, ...), condition=%wide.region_15.15_spmd.clone, body=%wide.region_13.14_spmd.clone.sunk | while | flops 341147136 | bytes 18110612 | solution.py:197
  630.7 16.1 %while.58 = (s32[]{:T(128)}, f32[1024,64]{0,1:T(8,128)}, f32[1024,64]{0,1:T(8,128)}, bf16[2,512,64]{1,2,0:T(8,128)(2,1)S(1)}, s32[2,512]{1,0:T(2,128)S(1)}, /*in...) while((s32[]{:T(128)}, f32[1024,64]{0,1:T(8,128)}, ...), condition=%wide.region_15.15_spmd.clone, body=%wide.region_13.14_spmd.clone.sunk | while | flops 341147136 | bytes 18110612 | solution.py:197
  649.8 2.5 convert_reduce_fusion.4
  652.6 8.2 fusion.62
  660.8 7.0 fusion.43
  667.8 3.8 copy.79
  671.6 2.6 fusion.38
  676.6 3.3 convert_reduce_fusion.2
  680.0 9.7 copy.107
  691.2 8.0 reshape.209
  699.3 10.2 fusion.65
  709.5 10.8 reshape.212
  720.3 584.6 %all-reduce.16 = (bf16[1769472]{0:T(1024)(128)(2,1)}, bf16[589824]{0:T(1024)(128)(2,1)}, bf16[2359296]{0:T(1024)(128)(2,1)}, bf16[2359296]{0:T(1024)(128)(2,1)},...) all-reduce(f32[1769472]{0:T(1024)} %reshape.209, ...), channel_id=2, replica_groups=mesh['fsdp'=16,'rep'=2] {'fsdp'}, use_global_device_ids=true, to_apply=%region_19.20.clone | all-reduce | flops 7087104 | bytes 42522624
  1311.4 9.5 add_convert_fusion.1
  1321.1 6.7 all-reduce.10
  1328.9 3.7 copy.83
  1334.1 24.2 %all-reduce.15.cloned.1.call-done = (bf16[110592]{0:T(1024)(128)(2,1)}, bf16[36864]{0:T(1024)(128)(2,1)}, bf16[147456]{0:T(1024)(128)(2,1)}, bf16[147456]{0:T(1024)(128)(2,1)}) async-done(((bf16[110592]{0:T(1024)(128)(2,1)}, bf16[36864]{0:T(1024)(128)(2,1)}, bf16[147456]{0:T(1024)(128)(2,1)}, bf16[147456]{0:T(1024)(128)(2,1)}), (bf16[110592]{0:T(1024)(128)(2,1)}, bf16[36864]{0:T(1024)(128)(2,1)}, ...) | async-done | bytes 884752 | tf_op jit(solution)/shard_map/psum | solution.py:249
  (752 shorter events, 440.2 us)
Async XLA Ops:
  7.2 61.5 %all-gather.7.cloned.1.call-start = ((), (), s32[]{:S(2)}) async-start(), calls=%async_computation.1 | async-start | bytes 1253376 | tf_op jit(solution)/shard_map/all_gather | solution.py:81
  7.9 89.8 %all-gather.5.cloned.1.call-start = ((), (), s32[]{:S(2)}) async-start(), calls=%async_computation | async-start | bytes 3760128 | tf_op jit(solution)/shard_map/all_gather | solution.py:80
  8.6 218.7 %all-gather.9.cloned.1.call-start = ((), (), s32[]{:S(2)}) async-start(), calls=%async_computation.2 | async-start | bytes 5013504 | tf_op jit(solution)/shard_map/all_gather | solution.py:82
  9.4 264.1 %all-gather.11.cloned.1.call-start = ((), (), s32[]{:S(2)}) async-start(), calls=%async_computation.3 | async-start | bytes 5013504 | tf_op jit(solution)/shard_map/all_gather | solution.py:83
  10.0 1348.3 %all-reduce.15.cloned.1.call-start = ((), (), s32[]{:S(2)}) async-start(), calls=%async_computation.4 | async-start | bytes 1769472 | tf_op jit(solution)/shard_map/psum | solution.py:249
  60.5 44.7 %copy-start.38 = (f32[768]{0:T(1024)}, f32[768]{0:T(1024)S(1)}, u32[]{:S(2)}) copy-start(f32[768]{0:T(1024)S(1)} %get-tuple-element.443) | copy-start | bytes 9220
  60.5 3.2 copy-start.14
  60.5 3.2 copy-start.17
  62.4 42.9 %copy-start = (bf16[1024,768]{0,1:T(8,128)(2,1)}, bf16[1024,768]{0,1:T(8,128)(2,1)S(1)}, u32[]{:S(2)}) copy-start(bf16[1024,768]{0,1:T(8,128)(2,1)S(1)} %copy.61) | copy-start | bytes 4718596
  62.7 42.6 %copy-start.23 = (f32[1024]{0:T(1024)}, f32[1024]{0:T(1024)S(1)}, u32[]{:S(2)}) copy-start(f32[1024]{0:T(1024)S(1)} %broadcast_multiply_fusion.1) | copy-start | bytes 12292
  63.1 0.6 copy-start.31
  63.2 42.1 %copy-start.27 = (f32[1024]{0:T(1024)}, f32[1024]{0:T(1024)S(1)}, u32[]{:S(2)}) copy-start(f32[1024]{0:T(1024)S(1)} %fusion.46) | copy-start | bytes 12292
  63.7 41.5 %copy-start.25 = (f32[768]{0:T(1024)}, f32[768]{0:T(1024)S(1)}, u32[]{:S(2)}) copy-start(f32[768]{0:T(1024)S(1)} %get-tuple-element.445) | copy-start | bytes 9220
  223.0 3.8 copy-start.12
  226.9 100.6 %copy-start.3 = (f32[1024,768]{0,1:T(8,128)}, f32[1024,768]{0,1:T(8,128)S(1)}, u32[]{:S(2)}) copy-start(f32[1024,768]{0,1:T(8,128)S(1)} %get-tuple-element.449) | copy-start | bytes 9437188
  302.0 10.5 copy-start.41
  323.9 3.5 copy-start.7
  327.5 1.4 copy-start.8
  328.4 1.7 copy-start.5
  328.4 1.6 copy-start.29
  328.9 1.9 copy-start.22
  330.7 1.4 copy-start.21
  337.7 4.1 copy-start.13
  337.7 4.1 copy-start.15
  649.7 2.5 copy-start.10
  649.7 2.8 copy-start.11
  652.6 8.2 copy-start.1
  652.6 8.2 copy-start.20
  652.6 8.2 copy-start.24
  652.6 8.2 copy-start.26
  652.6 8.2 copy-start.28
  652.6 8.2 copy-start.39
  671.6 2.6 copy-start.32
  671.6 2.8 copy-start.2
  674.2 1.9 copy-start.6
  674.2 2.4 copy-start.9
  674.2 2.4 copy-start.30
  676.6 3.3 copy-start.33
  676.6 3.3 copy-start.34
  676.6 3.3 copy-start.40
  676.6 3.4 copy-start.36
  676.6 3.4 copy-start.35
  680.0 9.7 copy-start.16
  691.2 8.0 copy-start.18
  720.3 591.1 %copy-start.4 = (f32[1024,768]{0,1:T(8,128)S(1)}, f32[1024,768]{0,1:T(8,128)}, u32[]{:S(2)}) copy-start(f32[1024,768]{0,1:T(8,128)} %copy-done.3) | copy-start | bytes 9437188
  720.3 591.1 %copy-start.37 = (f32[768]{0:T(1024)S(1)}, f32[768]{0:T(1024)}, u32[]{:S(2)}) copy-start(f32[768]{0:T(1024)} %get-tuple-element.438) | copy-start | bytes 9220
  1328.9 3.7 copy-start.19
Sparse Core Ops, SparseCore 0:
  10.3 37.7 all-gather.6
  50.4 47.2 all-gather.4
  100.0 51.6 all-gather.8
  153.8 51.6 all-gather.10
  1311.5 46.7 all-reduce.14
where the time goes:
time: 1390 us; the launch traced here: 1370 us
  blocking collectives  637 us (46%)
  matrix products  337 us (24%)
  local copies, waits for them, and re-layouts  279 us (20%)
  waiting for transfers between devices  52.4 us (4%)
  other arithmetic  44.7 us (3%)
  between operations  19.4 us (1%)
    unnamed x2, blocking collectives  630 us
    dot_general x76, matrix products, contract_last(): lax.dot_general(left, right, (((1,), (1,)), ((), ())), preferred_element_...  130 us
    dot_general x52, matrix products, contract_first(): lax.dot_general(left, right, (((0,), (0,)), ((), ())), preferred_element_...  124 us
    dynamic_update_slice x72, local copies, waits for them, and re-layouts, shards(): lax.map(head_forward, (query_heads, key_heads, value_heads))  57.3 us
    dynamic_slice x36, local copies, waits for them, and re-layouts, shards(): lax.map(head_forward, (query_heads, key_heads, value_heads))  51.8 us
    squeeze x36, local copies, waits for them, and re-layouts, shards(): lax.map(head_forward, (query_heads, key_heads, value_heads))  44.7 us
    dot_general x1, matrix products, shards(): jnp.dot(normed_two, weight_up, preferred_element_type=jnp.float32) + bias_up  37.7 us
    unnamed x106, local copies, waits for them, and re-layouts  31.4 us
  transfers between devices with their start and end apart: 5, of which 2 were waited for; matrix products, arithmetic and copies ran while one was open for 15% of the time, Pallas kernels for 0%

commit v1 on v0

v1 whole, which is shorter than its diff:
```python
import functools

import jax
import jax.numpy as jnp
from jax import lax
from jax.experimental import pallas as pl
from jax.experimental.pallas import tpu as pltpu
from jax.sharding import Mesh
from jax.sharding import PartitionSpec as P

D = 768
H = 12
HD = 64
FF = 3072
B16 = jnp.bfloat16
F32 = jnp.float32

epsilon_norm = 1e-06
score_scale = 0.125
masked_low = -1e30

FWD_GROUPS = (6, 6)
NZ, NX = 4, 2
ROWS = D // 16
ROWS2 = FF // 16
FSDP = ("z", "x", "core")


def mm(a, b, ca, cb):
    return lax.dot_general(a, b, (((ca,), (cb,)), ((), ())), preferred_element_type=F32)


def params(mib=56):
    return pltpu.CompilerParams(
        dimension_semantics=("arbitrary",), vmem_limit_bytes=mib * 1024 * 1024
    )


def cost(flops, nbytes, trans=0):
    return pl.CostEstimate(flops=int(flops), bytes_accessed=int(nbytes), transcendentals=int(trans))


def shape(dims, dtype):
    return jax.ShapeDtypeStruct(dims, dtype)


def layer_norm(values, gain, shift):
    center = values - jnp.mean(values, axis=-1, keepdims=True)
    spread = jnp.mean(center * center, axis=-1, keepdims=True)
    return center * lax.rsqrt(spread + epsilon_norm) * gain + shift


def layer_norm_back(values, gain, grad):
    center = values - jnp.mean(values, axis=-1, keepdims=True)
    spread = jnp.mean(center * center, axis=-1, keepdims=True)
    inverse = lax.rsqrt(spread + epsilon_norm)
    hat = center * inverse
    grad_hat = grad * gain
    grad_values = inverse * (
        grad_hat
        - jnp.mean(grad_hat, axis=-1, keepdims=True)
        - hat * jnp.mean(grad_hat * hat, axis=-1, keepdims=True)
    )
    return grad_values, jnp.sum(grad * hat, axis=0, keepdims=True), jnp.sum(grad, axis=0, keepdims=True)


def erf(x):
    x = jnp.clip(x, -3.7439211627767994, 3.7439211627767994)
    z = x * x
    top = 0.00022905065861350646
    for c in (0.0034082910107109506, 0.050955695062380861, 0.18520832239976145, 1.128379143519084):
        top = top * z + c
    low = -1.1791602954361697e-7
    for c in (
        0.000023547966471313185,
        0.0010179625278914885,
        0.014070470171167667,
        0.11098505178285362,
        0.49746925110067538,
        1.0,
    ):
        low = low * z + c
    return x * top / low


def block_of(tab, t):
    return tab[t]


def assemble(tab, mine, theirs, dest, rows):
    core = tab[8]
    for t in range(NZ * NX):
        base = tab[t] * 2
        dest[pl.ds(pl.multiple_of((base + core) * rows, 16), rows), :] = mine[t]
        dest[pl.ds(pl.multiple_of((base + 1 - core) * rows, 16), rows), :] = theirs[t]


def scatter(tab, source, own, send, rows):
    core = tab[8]
    for t in range(NZ * NX):
        base = tab[t] * 2
        own[t] = source[pl.ds(pl.multiple_of((base + core) * rows, 16), rows), :]
        send[t] = source[pl.ds(pl.multiple_of((base + 1 - core) * rows, 16), rows), :]


def qkv_body(first, tab, x_ref, mine, theirs, gain, shift, bias, *rest):
    if first:
        out_ref, h_ref, w_s = rest

        @pl.when(pl.program_id(0) == 0)
        def _():
            h_ref[...] = layer_norm(x_ref[...].astype(F32), gain[...], shift[...]).astype(B16)

        h = h_ref
    else:
        out_ref, w_s = rest
        h = x_ref
    assemble(tab, mine, theirs, w_s, ROWS)
    out_ref[0] = (mm(h[...], w_s[...], 1, 0) + bias[0]).astype(B16)


def qkv_call(first, tab, x, mine, theirs, gain, shift, bias):
    tokens = x.shape[0]
    width = mine.shape[2] // 3
    full = pl.BlockSpec((tokens, D), lambda j, t: (0, 0))
    row = pl.BlockSpec((1, D), lambda j, t: (0, 0))
    piece = pl.BlockSpec((8, ROWS, width), lambda j, t: (0, 0, j))
    outs = [shape((3, tokens, width), B16)]
    out_specs = [pl.BlockSpec((1, tokens, width), lambda j, t: (j, 0, 0))]
    if first:
        outs.append(shape((tokens, D), B16))
        out_specs.append(full)
    return pl.pallas_call(
        functools.partial(qkv_body, first),
        grid_spec=pltpu.PrefetchScalarGridSpec(
            num_scalar_prefetch=1,
            grid=(3,),
            in_specs=[full, piece, piece, row, row, pl.BlockSpec((1, 1, width), lambda j, t: (j, 0, 0))],
            out_specs=out_specs,
            scratch_shapes=[pltpu.VMEM((D, width), B16)],
        ),
        out_shape=outs,
        compiler_params=params(),
        cost_estimate=cost(6 * tokens * D * width, 8 * tokens * D),
        name="qkv_first" if first else "qkv_next",
    )(tab, x, mine, theirs, gain, shift, bias)


def make_mask(seg_ref, mask):
    @pl.when(pl.program_id(0) == 0)
    def _():
        row = seg_ref[...].astype(F32)
        mask[...] = jnp.where(row.T == row, 0.0, masked_low)


def attend_body(rows, q_ref, k_ref, v_ref, seg_ref, o_ref, lse_ref, mask):
    make_mask(seg_ref, mask)
    tokens = q_ref.shape[1]
    for h in range(2):
        cols = slice(h * HD, (h + 1) * HD)
        k = k_ref[0, :, cols]
        v = v_ref[0, :, cols]
        for b in range(tokens // rows):
            r = slice(b * rows, (b + 1) * rows)
            q = q_ref[0, r, cols] * jnp.asarray(score_scale, B16)
            s = mm(q, k, 1, 1) + mask[r, :]
            top = jnp.max(s, axis=-1, keepdims=True)
            p = jnp.exp(s - top)
            total = jnp.sum(p, axis=-1, keepdims=True)
            a = (p * (1.0 / total)).astype(B16)
            o_ref[r, cols] = mm(a, v, 1, 0).astype(B16)
            lse_ref[0, h : h + 1, r] = (top + jnp.log(total)).T


def attend_call(qkv, seg):
    _, tokens, width = qkv.shape
    pairs = width // 128
    head = lambda j: pl.BlockSpec((1, tokens, 128), lambda i: (j, 0, i))
    return pl.pallas_call(
        functools.partial(attend_body, min(512, tokens)),
        grid=(pairs,),
        in_specs=[head(0), head(1), head(2), pl.BlockSpec((1, tokens), lambda i: (0, 0))],
        out_specs=[
            pl.BlockSpec((tokens, 128), lambda i: (0, i)),
            pl.BlockSpec((1, 2, tokens), lambda i: (i, 0, 0)),
        ],
        out_shape=[shape((tokens, width), B16), shape((pairs, 2, tokens), F32)],
        scratch_shapes=[pltpu.VMEM((tokens, tokens), F32)],
        compiler_params=params(),
        cost_estimate=cost(pairs * 16 * 128 * tokens * tokens, 8 * tokens * width, pairs * 2 * tokens * tokens),
        name="attend",
    )(qkv, qkv, qkv, seg)


def up_body(split, tab, oa_ref, ob_ref, x_ref, mine, theirs, bo, gain, shift, c1, x1_ref, h2_ref, act_ref, slope_ref, wo, w1):
    @pl.when(pl.program_id(0) == 0)
    def _():
        core = tab[8]
        for t in range(NZ * NX):
            base = tab[t] * 2
            at = pl.ds(pl.multiple_of((base + core) * ROWS, 16), ROWS)
            wo[at, :] = mine[t, :, :D]
            w1[at, :] = mine[t, :, D:]
            at = pl.ds(pl.multiple_of((base + 1 - core) * ROWS, 16), ROWS)
            wo[at, :] = theirs[t, :, :D]
            w1[at, :] = theirs[t, :, D:]

    x1 = (
        x_ref[...].astype(F32)
        + (mm(oa_ref[...], wo[:split, :], 1, 0) + mm(ob_ref[...], wo[split:, :], 1, 0))
        + bo[...]
    )
    x1_ref[...] = x1
    h2 = layer_norm(x1, gain[...], shift[...]).astype(B16)
    h2_ref[...] = h2
    tile = 512
    for f in range(FF // tile):
        cols = slice(f * tile, (f + 1) * tile)
        u = mm(h2, w1[:, cols], 1, 0) + c1[:, cols]
        cdf = 0.5 + 0.5 * erf(u * 0.7071067811865476)
        act_ref[:, cols] = (u * cdf).astype(B16)
        slope_ref[:, cols] = (cdf + u * (jnp.exp(u * u * -0.5) * 0.3989422804014327)).astype(B16)


def up_call(tab, oa, ob, x, mine, theirs, bo, gain, shift, c1):
    tokens = x.shape[0]
    rows = min(256, tokens)
    split = oa.shape[1]
    block = lambda w: pl.BlockSpec((rows, w), lambda i, t: (i, 0))
    row = lambda w: pl.BlockSpec((1, w), lambda i, t: (0, 0))
    piece = pl.BlockSpec((8, ROWS, D + FF), lambda i, t: (0, 0, 0), pipeline_mode=pl.Buffered(1))
    return pl.pallas_call(
        functools.partial(up_body, split),
        grid_spec=pltpu.PrefetchScalarGridSpec(
            num_scalar_prefetch=1,
            grid=(tokens // rows,),
            in_specs=[block(split), block(D - split), block(D), piece, piece, row(D), row(D), row(D), row(FF)],
            out_specs=[block(D), block(D), block(FF), block(FF)],
            scratch_shapes=[pltpu.VMEM((D, D), B16), pltpu.VMEM((D, FF), B16)],
        ),
        out_shape=[shape((tokens, D), F32), shape((tokens, D), B16), shape((tokens, FF), B16), shape((tokens, FF), B16)],
        compiler_params=params(),
        cost_estimate=cost(2 * tokens * D * (D + FF), 30 * tokens * D, tokens * FF),
        name="up",
    )(tab, oa, ob, x, mine, theirs, bo, gain, shift, c1)


def down_body(tab, act_ref, slope_ref, dy_ref, x1_ref, mine, theirs, c2, out_ref, du_ref, own, send, dc1, dc2, acc, w2, dw2):
    step = pl.program_id(0)
    core = tab[8]

    @pl.when(step == 0)
    def _():
        acc[...] = x1_ref[...] + c2[...]
        dc2[...] = jnp.sum(dy_ref[...].astype(F32), axis=0, keepdims=True)

    for rx in range(NX):
        base = lax.rem(tab[rx * NZ], 2) * 2
        w2[pl.ds(pl.multiple_of((base + core) * ROWS2, 64), ROWS2), :] = mine[rx, 0]
        w2[pl.ds(pl.multiple_of((base + 1 - core) * ROWS2, 64), ROWS2), :] = theirs[rx, 0]
    act = act_ref[...]
    dy = dy_ref[...]
    w = w2[...]
    du = (mm(dy, w, 1, 1) * slope_ref[...].astype(F32)).astype(B16)
    du_ref[...] = du
    dc1[...] = jnp.sum(du.astype(F32), axis=0, keepdims=True)
    acc[...] += mm(act, w, 1, 0)
    dw2[...] = mm(act, dy, 0, 0).astype(B16)
    for rx in range(NX):
        base = lax.rem(tab[rx * NZ], 2) * 2
        own[rx, 0] = dw2[pl.ds(pl.multiple_of((base + core) * ROWS2, 64), ROWS2), :]
        send[rx, 0] = dw2[pl.ds(pl.multiple_of((base + 1 - core) * ROWS2, 64), ROWS2), :]

    @pl.when(step == NZ - 1)
    def _():
        out_ref[...] = acc[...].astype(B16)


def down_call(tab, act, slope, dy, x1, mine, theirs, c2):
    tokens = dy.shape[0]
    width = FF // NZ
    full = pl.BlockSpec((tokens, D), lambda i, t: (0, 0))
    ff = pl.BlockSpec((tokens, width), lambda i, t: (0, t[i] // 2))
    piece = pl.BlockSpec((NX, 1, ROWS2, D), lambda i, t: (0, i, 0, 0))
    row = pl.BlockSpec((1, D), lambda i, t: (0, 0))
    pieces = shape((NX, NZ, ROWS2, D), B16)
    return pl.pallas_call(
        down_body,
        grid_spec=pltpu.PrefetchScalarGridSpec(
            num_scalar_prefetch=1,
            grid=(NZ,),
            in_specs=[ff, ff, full, full, piece, piece, row],
            out_specs=[full, ff, piece, piece, pl.BlockSpec((1, width), lambda i, t: (0, t[i] // 2)), row],
            scratch_shapes=[pltpu.VMEM((tokens, D), F32), pltpu.VMEM((width, D), B16), pltpu.VMEM((width, D), B16)],
        ),
        out_shape=[
            shape((tokens, D), B16),
            shape((tokens, FF), B16),
            pieces,
            pieces,
            shape((1, FF), F32),
            shape((1, D), F32),
        ],
        compiler_params=params(),
        cost_estimate=cost(6 * tokens * D * FF, 40 * tokens * D),
        name="down",
    )(tab, act, slope, dy, x1, mine.reshape(NX, NZ, ROWS2, D), theirs.reshape(NX, NZ, ROWS2, D), c2)


def middle_body(split, tab, h2_ref, du_ref, dy_ref, x1_ref, oa_ref, ob_ref, mine, theirs, gain, dx_ref, do_ref, own, send, dvec, acc, w_s, dw):
    step = pl.program_id(0)

    @pl.when(step == 0)
    def _():
        acc[...] = jnp.zeros_like(acc)

    assemble(tab, mine, theirs, w_s, ROWS)

    @pl.when(step < NZ)
    def _():
        du = du_ref[...]
        dw[...] = mm(h2_ref[...], du, 0, 0).astype(B16)
        acc[...] += mm(du, w_s[...], 1, 1)

    @pl.when(step == NZ)
    def _():
        grad, dgain, dshift = layer_norm_back(x1_ref[...], gain[...], acc[...])
        dx = dy_ref[...].astype(F32) + grad
        dx_ref[...] = dx
        da = dx.astype(B16)
        dvec[0:1, :] = dgain
        dvec[1:2, :] = dshift
        dvec[2:3, :] = jnp.sum(da.astype(F32), axis=0, keepdims=True)
        do_ref[...] = mm(da, w_s[...], 1, 1).astype(B16)
        dw[:split, :] = mm(oa_ref[...], da, 0, 0).astype(B16)
        dw[split:, :] = mm(ob_ref[...], da, 0, 0).astype(B16)

    scatter(tab, dw, own, send, ROWS)


def middle_call(tab, h2, du, dy, x1, oa, ob, mine, theirs, gain):
    tokens = dy.shape[0]
    split = oa.shape[1]
    full = lambda w: pl.BlockSpec((tokens, w), lambda i, t: (0, 0), pipeline_mode=pl.Buffered(1))
    out_full = pl.BlockSpec((tokens, D), lambda i, t: (0, 0))
    piece = pl.BlockSpec((8, ROWS, D), lambda i, t: (0, 0, lax.rem(i + 1, NZ + 1)))
    pieces = shape((8, ROWS, D + FF), B16)
    return pl.pallas_call(
        functools.partial(middle_body, split),
        grid_spec=pltpu.PrefetchScalarGridSpec(
            num_scalar_prefetch=1,
            grid=(NZ + 1,),
            in_specs=[
                full(D),
                pl.BlockSpec((tokens, D), lambda i, t: (0, jnp.minimum(i, NZ - 1))),
                full(D),
                full(D),
                full(split),
                full(D - split),
                piece,
                piece,
                pl.BlockSpec((1, D), lambda i, t: (0, 0)),
            ],
            out_specs=[out_full, out_full, piece, piece, pl.BlockSpec((8, D), lambda i, t: (0, 0))],
            scratch_shapes=[pltpu.VMEM((tokens, D), F32), pltpu.VMEM((D, D), B16), pltpu.VMEM((D, D), B16)],
        ),
        out_shape=[shape((tokens, D), F32), shape((tokens, D), B16), pieces, pieces, shape((8, D), F32)],
        compiler_params=params(),
        cost_estimate=cost(4 * tokens * D * (D + FF), 40 * tokens * D),
        name="middle",
    )(tab, h2, du, dy, x1, oa, ob, mine, theirs, gain)


def attend_back_body(rows, q_ref, k_ref, v_ref, do_ref, o_ref, lse_ref, seg_ref, out_ref, mask):
    make_mask(seg_ref, mask)
    tokens = q_ref.shape[1]
    for h in range(2):
        cols = slice(h * HD, (h + 1) * HD)
        k = k_ref[0, :, cols]
        v = v_ref[0, :, cols]
        dk = jnp.zeros((HD, tokens), F32)
        dv = jnp.zeros((HD, tokens), F32)
        for b in range(tokens // rows):
            r = slice(b * rows, (b + 1) * rows)
            q = q_ref[0, r, cols] * jnp.asarray(score_scale, B16)
            do = do_ref[r, cols]
            centre = jnp.sum(do.astype(F32) * o_ref[r, cols].astype(F32), axis=1, keepdims=True)
            s = mm(q, k, 1, 1) + mask[r, :]
            p = jnp.exp(s - lse_ref[0, h : h + 1, r].T)
            da = mm(do, v, 1, 1)
            ds = (p * (da - centre)).astype(B16)
            dv = dv + mm(do.T, p.astype(B16), 1, 0)
            dk = dk + mm(q.T, ds, 1, 0)
            out_ref[0, r, cols] = (mm(ds, k, 1, 0) * score_scale).astype(B16)
        out_ref[1, :, cols] = dk.T.astype(B16)
        out_ref[2, :, cols] = dv.T.astype(B16)


def attend_back_call(qkv, do, o, lse, seg, first_pair):
    _, tokens, width = qkv.shape
    pairs = width // 128
    head = lambda j: pl.BlockSpec((1, tokens, 128), lambda i: (j, 0, i))
    return pl.pallas_call(
        functools.partial(attend_back_body, min(512, tokens)),
        grid=(pairs,),
        in_specs=[
            head(0),
            head(1),
            head(2),
            pl.BlockSpec((tokens, 128), lambda i: (0, i + first_pair)),
            pl.BlockSpec((tokens, 128), lambda i: (0, i)),
            pl.BlockSpec((1, 2, tokens), lambda i: (i, 0, 0)),
            pl.BlockSpec((1, tokens), lambda i: (0, 0)),
        ],
        out_specs=pl.BlockSpec((3, tokens, 128), lambda i: (0, 0, i)),
        out_shape=shape((3, tokens, width), B16),
        scratch_shapes=[pltpu.VMEM((tokens, tokens), F32)],
        compiler_params=params(),
        cost_estimate=cost(pairs * 40 * 128 * tokens * tokens, 16 * tokens * width, pairs * 2 * tokens * tokens),
        name="attend_back",
    )(qkv, qkv, qkv, do, o, lse, seg)


def weight_body(tab, h_ref, d_ref, own, send, dbias, dw):
    d = d_ref[0]
    dbias[0] = jnp.sum(d.astype(F32), axis=0, keepdims=True)
    dw[...] = mm(h_ref[...], d, 0, 0).astype(B16)
    scatter(tab, dw, own, send, ROWS)


def weight_call(tab, h1, dqkv):
    _, tokens, width = dqkv.shape
    piece = pl.BlockSpec((8, ROWS, width), lambda j, t: (0, 0, j))
    pieces = shape((8, ROWS, 3 * width), B16)
    return pl.pallas_call(
        weight_body,
        grid_spec=pltpu.PrefetchScalarGridSpec(
            num_scalar_prefetch=1,
            grid=(3,),
            in_specs=[
                pl.BlockSpec((tokens, D), lambda j, t: (0, 0)),
                pl.BlockSpec((1, tokens, width), lambda j, t: (j, 0, 0)),
            ],
            out_specs=[piece, piece, pl.BlockSpec((1, 1, width), lambda j, t: (j, 0, 0))],
            scratch_shapes=[pltpu.VMEM((D, width), B16)],
        ),
        out_shape=[pieces, pieces, shape((3, 1, width), F32)],
        compiler_params=params(),
        cost_estimate=cost(6 * tokens * D * width, 12 * tokens * width),
        name="qkv_weight",
    )(tab, h1, dqkv)


def input_body(tab, da_ref, db_ref, x_ref, dx_ref, ma, ta, mb, tb, gain, out_ref, dvec, wa, wb):
    step = pl.program_id(0)

    @pl.when(step == 0)
    def _():
        assemble(tab, ma, ta, wa, ROWS)
        assemble(tab, mb, tb, wb, ROWS)
        dvec[...] = jnp.zeros_like(dvec)

    dh = None
    for d_ref, w in ((da_ref, wa), (db_ref, wb)):
        width = d_ref.shape[2]
        for j in range(3):
            term = mm(d_ref[j], w[:, j * width : (j + 1) * width], 1, 1)
            dh = term if dh is None else dh + term
    grad, dgain, dshift = layer_norm_back(x_ref[...].astype(F32), gain[...], dh)
    out_ref[...] = dx_ref[...] + grad
    dvec[0:1, :] += dgain
    dvec[1:2, :] += dshift


def input_call(tab, da, db, x, dx, ma, ta, mb, tb, gain):
    tokens = x.shape[0]
    rows = min(256, tokens)
    wa, wb = da.shape[2], db.shape[2]
    grads = lambda w: pl.BlockSpec((3, rows, w), lambda i, t: (0, i, 0))
    block = pl.BlockSpec((rows, D), lambda i, t: (i, 0))
    piece = lambda w: pl.BlockSpec((8, ROWS, 3 * w), lambda i, t: (0, 0, 0), pipeline_mode=pl.Buffered(1))
    return pl.pallas_call(
        input_body,
        grid_spec=pltpu.PrefetchScalarGridSpec(
            num_scalar_prefetch=1,
            grid=(tokens // rows,),
            in_specs=[
                grads(wa),
                grads(wb),
                block,
                block,
                piece(wa),
                piece(wa),
                piece(wb),
                piece(wb),
                pl.BlockSpec((1, D), lambda i, t: (0, 0)),
            ],
            out_specs=[block, pl.BlockSpec((8, D), lambda i, t: (0, 0))],
            scratch_shapes=[pltpu.VMEM((D, 3 * wa), B16), pltpu.VMEM((D, 3 * wb), B16)],
        ),
        out_shape=[shape((tokens, D), F32), shape((8, D), F32)],
        compiler_params=params(),
        cost_estimate=cost(6 * tokens * D * D, 20 * tokens * D),
        name="input_grad",
    )(tab, da, db, x, dx, ma, ta, mb, tb, gain)


def add_core_body(a, b, keep, send):
    keep[0] = (a[0, 0].astype(F32) + b[0, 0].astype(F32)).astype(B16)
    send[0] = (a[1, 0].astype(F32) + b[1, 0].astype(F32)).astype(B16)


def add_core(own, received):
    _, r, w = own.shape
    both = pl.BlockSpec((NX, 1, r, w), lambda i: (0, i, 0, 0))
    one = pl.BlockSpec((1, r, w), lambda i: (i, 0, 0))
    return pl.pallas_call(
        add_core_body,
        grid=(NZ,),
        in_specs=[both, both],
        out_specs=[one, one],
        out_shape=[shape((NZ, r, w), B16)] * 2,
        compiler_params=params(),
        cost_estimate=cost(8 * r * w, 48 * r * w),
        name="add_core",
    )(own.reshape(NX, NZ, r, w), received.reshape(NX, NZ, r, w))


def add_x_body(a, b, *outs):
    for i, out in enumerate(outs):
        out[...] = (a[i].astype(F32) + b[i].astype(F32)).astype(B16)


def add_x(keep, received):
    _, r, w = keep.shape
    return pl.pallas_call(
        add_x_body,
        out_shape=[shape((r, w), B16)] * NZ,
        compiler_params=pltpu.CompilerParams(vmem_limit_bytes=32 * 1024 * 1024),
        cost_estimate=cost(4 * r * w, 24 * r * w),
        name="add_x",
    )(keep, received)


def add_z_body(a, b, c, d, out):
    out[...] = ((a[...].astype(F32) + b[...].astype(F32)) + (c[...].astype(F32) + d[...].astype(F32))).astype(B16)


def add_z(parts):
    return pl.pallas_call(
        add_z_body,
        out_shape=shape(parts[0].shape, B16),
        compiler_params=pltpu.CompilerParams(vmem_limit_bytes=32 * 1024 * 1024),
        cost_estimate=cost(4 * parts[0].size, 10 * parts[0].size),
        name="add_z",
    )(*parts)


def flip(value, axis, size, by):
    return lax.ppermute(value, axis, [(i, i ^ by) for i in range(size)])


def gather_blocks(shard):
    along = jnp.stack([shard] + [flip(shard, "z", NZ, by) for by in range(1, NZ)])
    mine = jnp.concatenate([along, flip(along, "x", NX, 1)])
    return mine, flip(mine, "core", 2, 1)


def reduce_blocks(own, send):
    keep, out = add_core(own, flip(send, "core", 2, 1))
    parts = add_x(keep, flip(out, "x", NX, 1))
    total = add_z([parts[0]] + [flip(parts[by], "z", NZ, by) for by in range(1, NZ)])
    return total.astype(F32) + flip(total, "rep", 2, 1).astype(F32)


def gather_any(shard):
    whole = lax.all_gather(shard, FSDP, axis=0, tiled=True)
    blocks = whole.reshape(NZ, NX, 2, -1, whole.shape[1]).transpose(2, 1, 0, 3, 4)
    blocks = blocks.reshape(2, NZ * NX, -1, whole.shape[1])
    return blocks[0], blocks[1]


def reduce_any(own, send):
    blocks = jnp.stack([own, send]).reshape(2, NX, NZ, *own.shape[1:]).transpose(2, 1, 0, 3, 4)
    whole = blocks.reshape(-1, own.shape[2])
    part = lax.psum_scatter(whole, FSDP, scatter_dimension=0, tiled=True)
    return lax.psum(part, "rep").astype(F32)


def shards(tokens, w_qkv, w_out, w_fc1, w_fc2, gains, biases, segment, cotangent):
    nz, nx = lax.axis_size("z"), lax.axis_size("x")
    count = nz * nx * 2
    grid = (nz, nx, lax.axis_size("core"), lax.axis_size("rep")) == (NZ, NX, 2, 2)
    gather, reduce = (gather_blocks, reduce_blocks) if grid else (gather_any, reduce_any)
    if grid:
        mz, mx, core = lax.axis_index("z"), lax.axis_index("x"), lax.axis_index("core")
    else:
        mz, mx, core = 0, 0, 0
    tab = jnp.stack(
        [jnp.asarray((mz ^ rz) * NX + (mx ^ rx), jnp.int32) for rx in range(NX) for rz in range(NZ)]
        + [jnp.asarray(core, jnp.int32)]
    )
    seg = segment.reshape(1, -1)

    shard_qkv = w_qkv.reshape(-1, 3 * D)
    bounds = []
    at = 0
    for heads in FWD_GROUPS:
        bounds.append((at * HD, (at + heads) * HD))
        at += heads
    qkv_shards = [
        jnp.concatenate([shard_qkv[:, part * D + a : part * D + b] for part in range(3)], axis=1)
        for a, b in bounds
    ]
    qkv_pieces = [gather(s) for s in qkv_shards]
    vec = jnp.concatenate([gains, biases])
    vec = lax.all_to_all(
        jnp.broadcast_to(vec[None], (count, vec.shape[0])), FSDP, split_axis=0, concat_axis=0, tiled=True
    ).astype(F32)
    ngain = gains.shape[0]
    gains_all = vec[:, :ngain].reshape(1, -1)
    biases_all = vec[:, ngain:].reshape(1, -1)
    gain_one, gain_two = gains_all[:, :D], gains_all[:, D:]
    shift_one, bias_q, bias_v, bias_o, shift_two = [biases_all[:, i * D : (i + 1) * D] for i in range(5)]
    bias_up, bias_down = biases_all[:, 5 * D : 5 * D + FF], biases_all[:, 5 * D + FF :]
    shard_up = jnp.concatenate([w_out.reshape(-1, D), w_fc1.reshape(-1, FF)], axis=1)
    up_mine, up_theirs = gather(shard_up)
    down_mine, down_theirs = gather(w_fc2.reshape(-1, D))

    qkv, outs, lses = [], [], []
    h1 = None
    for g, (a, b) in enumerate(bounds):
        bias = jnp.stack([bias_q[:, a:b], jnp.zeros((1, b - a), F32), bias_v[:, a:b]])
        mine, theirs = qkv_pieces[g]
        if g == 0:
            proj, h1 = qkv_call(True, tab, tokens, mine, theirs, gain_one, shift_one, bias)
        else:
            (proj,) = qkv_call(False, tab, h1, mine, theirs, gain_one, shift_one, bias)
        o, lse = attend_call(proj, seg)
        qkv.append(proj)
        outs.append(o)
        lses.append(lse)
    x1, h2, act, slope = up_call(
        tab, outs[0], outs[1], tokens, up_mine, up_theirs, bias_o, gain_two, shift_two, bias_up
    )
    output, du, own2, send2, dc1, dc2 = down_call(
        tab, act, slope, cotangent, x1, down_mine, down_theirs, bias_down
    )
    grad_fc2 = reduce(own2.reshape(8, ROWS2, D), send2.reshape(8, ROWS2, D))
    dx1, do, own1, send1, dmid = middle_call(
        tab, h2, du, cotangent, x1, outs[0], outs[1], up_mine, up_theirs, gain_two
    )
    grad_up = reduce(own1, send1)
    dqkv, grads, dbias = [], [], []
    for g, (a, b) in enumerate(bounds):
        d = attend_back_call(qkv[g], do, outs[g], lses[g], seg, a // 128)
        own, send, db = weight_call(tab, h1, d)
        grads.append(reduce(own, send))
        dqkv.append(d)
        dbias.append(db)
    grad_tokens, din = input_call(
        tab, dqkv[0], dqkv[1], tokens, dx1, *qkv_pieces[0], *qkv_pieces[1], gain_one
    )
    dgains = jnp.concatenate([din[0], dmid[0]])
    dbiases = jnp.concatenate(
        [
            din[1],
            jnp.concatenate([db[0, 0] for db in dbias]),
            jnp.concatenate([db[2, 0] for db in dbias]),
            dmid[2],
            dmid[1],
            dc1[0],
            dc2[0],
        ]
    )
    small = jnp.concatenate([dgains.reshape(count, -1), dbiases.reshape(count, -1)], axis=1)
    reps = lax.axis_size("rep")
    small = jnp.broadcast_to(small[:, None], (count, reps, small.shape[1])).reshape(count * reps, -1)
    small = lax.all_to_all(small, FSDP + ("rep",), split_axis=0, concat_axis=0, tiled=True)
    small = jnp.sum(small, axis=0)
    widths = [b - a for a, b in bounds]
    grad_qkv = jnp.concatenate(
        [g[:, part * w : (part + 1) * w] for part in range(3) for g, w in zip(grads, widths)], axis=1
    )
    return (
        output,
        grad_tokens,
        grad_qkv.reshape(-1),
        grad_up[:, :D].reshape(-1),
        grad_up[:, D:].reshape(-1),
        grad_fc2.reshape(-1),
        small[:ngain],
        small[ngain:],
    )


def solution(mesh):
    count, reps = mesh.shape["fsdp"], mesh.shape["rep"]
    inner = Mesh(mesh.devices.reshape(count // 4, 2, 2, reps), FSDP + ("rep",))
    rows = P(FSDP + ("rep",), None)
    flat = P(FSDP)
    return jax.shard_map(
        shards,
        mesh=inner,
        in_specs=(rows, flat, flat, flat, flat, flat, flat, P(FSDP + ("rep",)), rows),
        out_specs=(rows, rows, flat, flat, flat, flat, flat, flat),
        check_vma=False,
    )
```

time: 1390 us -> 510 us (0.37)
  blocking collectives: 637 us -> 0 us
  matrix products: 337 us -> 0 us
  local copies, waits for them, and re-layouts: 279 us -> 26.4 us
  Pallas kernels: 0 us -> 204 us
  waiting for transfers between devices: 52.4 us -> 204 us
  starting transfers between devices: 0.19 us -> 60 us
  other arithmetic: 44.7 us -> 3.71 us
  between operations: 19.4 us -> 1.68 us
    unnamed x2 -> x0, blocking collectives: 630 us -> none
    dot_general x180 -> x0, matrix products: 337 us -> none  [the longest x76 130 us: contract_last(): lax.dot_general(left, right, (((1,), (1,)), ((), ())), preferred_element_...]
    pallas_call x0 -> x24, Pallas kernels: none -> 204 us  [the longest x2 37.5 us: attend_back_call(): pl.pallas_call(functools.partial(attend_back_body, min(512, tokens)), gri...]
    ppermute x0 -> x44, waiting for transfers between devices: none -> 204 us  [flip(): return lax.ppermute(value, axis, [(i, i ^ by) for i in range(size)])]
    dynamic_slice x120 -> x0, local copies, waits for them, and re-layouts: 61.8 us -> none  [the longest x36 51.8 us: shards(): lax.map(head_forward, (query_heads, key_heads, value_heads))]
    dynamic_update_slice x96 -> x0, local copies, waits for them, and re-layouts: 58.3 us -> none  [the longest x72 57.3 us: shards(): lax.map(head_forward, (query_heads, key_heads, value_heads))]
    ppermute x0 -> x44, starting transfers between devices: none -> 47.6 us  [flip(): return lax.ppermute(value, axis, [(i, i ^ by) for i in range(size)])]
    reshape x21 -> x10, local copies, waits for them, and re-layouts: 52.3 us -> 5.22 us  [the longest x1 1.27 us: shards(): shard_qkv = w_qkv.reshape(-1, 3 * D)]
  transfers between devices with their start and end apart: 5 -> 46, of which waited for: 2 -> 14; matrix products, arithmetic and copies ran while one was open for 15% -> 4% of each run, Pallas kernels for 0% -> 36%
where the time goes in v1:
time: 510 us; the launch traced here: 500 us
  waiting for transfers between devices  204 us (40%)
  Pallas kernels  204 us (40%)
  starting transfers between devices  60 us (12%)
  local copies, waits for them, and re-layouts  26.4 us (5%)
    ppermute x44, waiting for transfers between devices, flip(): return lax.ppermute(value, axis, [(i, i ^ by) for i in range(size)])  204 us
    ppermute x44, starting transfers between devices, flip(): return lax.ppermute(value, axis, [(i, i ^ by) for i in range(size)])  47.6 us
    pallas_call x2, Pallas kernels, attend_back_call(): pl.pallas_call(functools.partial(attend_back_body, min(512, tokens)), gri...  37.5 us
    pallas_call x2, Pallas kernels, attend_call(): pl.pallas_call(functools.partial(attend_body, min(512, tokens)), grid=(pa...  31.3 us
    pallas_call x1, Pallas kernels, up_call(): pl.pallas_call(functools.partial(up_body, split), grid_spec=pltpu.Prefetc...  30 us
    pallas_call x1, Pallas kernels, down_call(): pl.pallas_call(down_body, grid_spec=pltpu.PrefetchScalarGridSpec(num_scal...  24.1 us
    pallas_call x1, Pallas kernels, middle_call(): pl.pallas_call(functools.partial(middle_body, split), grid_spec=pltpu.Pre...  24 us
    pallas_call x4, Pallas kernels, add_core(): pl.pallas_call(add_core_body, grid=(NZ,), in_specs=[both, both], out_spec...  16.4 us
  transfers between devices with their start and end apart: 46, of which 14 were waited for; matrix products, arithmetic and copies ran while one was open for 4% of the time, Pallas kernels for 36%

profile of v1, /device:TPU:16, one launch (start us, length us, event | category | flops | bytes accessed | tf_op | source)
XLA Modules:
  0.0 500.2 jit_solution(7041702641801779003)
XLA Ops:
  0.7 1.3 reshape.100
  2.0 1.6 collective-permute-start
  4.0 1.6 collective-permute-start.2
  5.6 2.5 collective-permute-start.5
  10.9 6.3 %all-to-all-start = ((bf16[16,2,288]{2,1,0:T(2,128)(2,1)}), bf16[16,2,288]{2,1,0:T(2,128)(2,1)S(1)}, u32[]{:S(2)}, u32[]{:S(2)}) async-start(bf16[16,2,288]{2,1,0:T(2,128)(2,1)} %reshape.134), calls=%async_computation | async-start | bytes 49152 | tf_op jit(solution)/shard_map/all_to_all | solution.py:617
  17.8 1.0 reshape.104
  22.8 1.1 collective-permute-start.7
  24.6 2.5 collective-permute-start.10
  28.7 2.0 collective-permute-start.15
  31.5 0.9 collective-permute-start.17
  32.6 24.6 %collective-permute-done.15 = bf16[192,768]{1,0:T(8,128)(2,1)S(1)} collective-permute-done((bf16[192,768]{1,0:T(8,128)(2,1)S(1)}, bf16[192,768]{1,0:T(8,128)(2,1)S(1)}, u32[]{:S(2)}, u32[]{:S(2)}) %collective-permute-start.15) | collective-permute-done | bytes 294944 | tf_op jit(solution)/shard_map/ppermute | solution.py:560
  57.7 14.2 %collective-permute-done.16 = bf16[192,768]{1,0:T(8,128)(2,1)S(1)} collective-permute-done((bf16[192,768]{1,0:T(8,128)(2,1)S(1)}, bf16[192,768]{1,0:T(8,128)(2,1)S(1)}, u32[]{:S(2)}, u32[]{:S(2)}) %collective-permute-start.16) | collective-permute-done | bytes 294944 | tf_op jit(solution)/shard_map/ppermute | solution.py:560
  71.9 1.4 collective-permute-start.3
  73.3 6.5 %collective-permute-done.17 = bf16[192,768]{1,0:T(8,128)(2,1)S(1)} collective-permute-done((bf16[192,768]{1,0:T(8,128)(2,1)S(1)}, bf16[192,768]{1,0:T(8,128)(2,1)S(1)}, u32[]{:S(2)}, u32[]{:S(2)}) %collective-permute-start.17) | collective-permute-done | bytes 294944 | tf_op jit(solution)/shard_map/ppermute | solution.py:560
  79.8 1.5 collective-permute-start.8
  82.7 4.5 collective-permute-done.12
  87.5 1.5 collective-permute-start.13
  89.1 58.9 %collective-permute-done.13 = bf16[4,48,3840]{2,1,0:T(8,128)(2,1)S(1)} collective-permute-done((bf16[4,48,3840]{2,1,0:T(8,128)(2,1)S(1)}, bf16[4,48,3840]{2,1,0:T(8,128)(2,1)S(1)}, u32[]{:S(2)}, u32[]{:S(2)}) %collective-permute-start.13) | collective-permute-done | bytes 1474592 | tf_op jit(solution)/shard_map/ppermute | solution.py:560
  150.6 1.1 constant_dynamic-update-slice_fusion.17
  153.8 1.0 collective-permute-done.4.theirs.ta
  154.8 0.9 copy-done.17
  155.7 7.9 %qkv_first.1 = (bf16[3,1024,384]{2,1,0:T(8,128)(2,1)}, bf16[1024,768]{1,0:T(8,128)(2,1)}) custom-call(s32[9]{0:T(128)} %stack.114.tab, bf16[1024,768]{1,0:T(8,128)(2,1)} %x_ref.5, bf16[8,48,1152]{2,1,0:T(8,128)(2,1)} %copy-done.12, bf16[8,48,1152]{2,1,0:T(8,128)(2,1)} %copy-done.17, f32[1,768]{1,0:T(1,128)} %get-tuple-element.142.gain, ...), custom_call_target="tpu_custom_call" | custom-call | flops 1811939328 | bytes 6291456 | tf_op jit(solution)/shard_map/qkv_first/pallas_call | solution.py:133
  163.6 0.9 copy-done.18
  164.6 6.7 %qkv_next.1.q_ref.k_ref.v_ref = bf16[3,1024,384]{2,1,0:T(8,128)(2,1)} custom-call(s32[9]{0:T(128)} %stack.114.tab, bf16[1024,768]{1,0:T(8,128)(2,1)} %get-tuple-element.63.x_ref.h_ref, bf16[8,48,1152]{2,1,0:T(8,128)(2,1)} %copy-done.10, bf16[8,48,1152]{2,1,0:T(8,128)(2,1)} %copy-done.18, f32[1,768]{1,0:T(1,128)} %get-tuple-element.142.gain, ...), custom_call_target="tpu_custom_call" | custom-call | flops 1811939328 | bytes 6291456 | tf_op jit(solution)/shard_map/qkv_next/pallas_call | solution.py:133
  171.3 15.4 %attend.3 = (bf16[1024,384]{1,0:T(8,128)(2,1)}, f32[3,2,1024]{2,1,0:T(2,128)}) custom-call(bf16[3,1024,384]{2,1,0:T(8,128)(2,1)} %qkv_next.1.q_ref.k_ref.v_ref, bf16[3,1024,384]{2,1,0:T(8,128)(2,1)} %qkv_next.1.q_ref.k_ref.v_ref, bf16[3,1024,384]{2,1,0:T(8,128)(2,1)} %qkv_next.1.q_ref.k_ref.v_ref, s32[1,1024]{1,0:T(1,128)} %bitcast.91), custom_call_target="tpu_custom_call" | custom-call | flops 6442450944 | bytes 3145728 | tf_op jit(solution)/shard_map/attend/pallas_call | solution.py:179
  186.7 15.9 %attend.2 = (bf16[1024,384]{1,0:T(8,128)(2,1)}, f32[3,2,1024]{2,1,0:T(2,128)}) custom-call(bf16[3,1024,384]{2,1,0:T(8,128)(2,1)} %get-tuple-element.61.q_ref.k_ref.v_ref, bf16[3,1024,384]{2,1,0:T(8,128)(2,1)} %get-tuple-element.61.q_ref.k_ref.v_ref, bf16[3,1024,384]{2,1,0:T(8,128)(2,1)} %get-tuple-element.61.q_ref.k_ref.v_ref, s32[1,1024]{1,0:T(1,128)} %bitcast.92), custom_call_target="tpu_custom_call" | custom-call | flops 6442450944 | bytes 3145728 | tf_op jit(solution)/shard_map/attend/pallas_call | solution.py:179
  202.6 30.0 %up.1 = (f32[1024,768]{1,0:T(8,128)}, bf16[1024,768]{1,0:T(8,128)(2,1)}, bf16[1024,3072]{1,0:T(8,128)(2,1)}, bf16[1024,3072]{1,0:T(8,128)(2,1)}) custom-call(s32[9]{0:T(128)} %stack.114.tab, bf16[1024,384]{1,0:T(8,128)(2,1)} %get-tuple-element.62.oa_ref.o_ref, bf16[1024,384]{1,0:T(8,128)(2,1)} %get-tuple-element.64.ob_ref.o_ref, bf16[1024,768]{1,0:T(8,128)(2,1)} %x_ref.5, ...), custom_call_target="tpu_custom_call" | custom-call | flops 6039797760 | bytes 23592960 | tf_op jit(solution)/shard_map/up/pallas_call | solution.py:232
  232.6 24.1 %down.1 = (bf16[1024,768]{1,0:T(8,128)(2,1)}, bf16[1024,3072]{1,0:T(8,128)(2,1)}, bf16[2,4,192,768]{3,2,1,0:T(8,128)(2,1)}, bf16[2,4,192,768]{3,2,1,0:T(8,128)(2...) custom-call(s32[9]{0:T(128)} %stack.114.tab, bf16[1024,3072]{1,0:T(8,128)(2,1)} %get-tuple-element.65.act_ref, ...), custom_call_target="tpu_custom_call" | custom-call | flops 14495514624 | bytes 31457280 | tf_op jit(solution)/shard_map/down/pallas_call | solution.py:287
  256.8 24.0 %middle.1 = (f32[1024,768]{1,0:T(8,128)}, bf16[1024,768]{1,0:T(8,128)(2,1)}, bf16[8,48,3840]{2,1,0:T(8,128)(2,1)}, bf16[8,48,3840]{2,1,0:T(8,128)(2,1)}, f32[8,768]{1,0:T(8,128)}) custom-call(s32[9]{0:T(128)} %stack.114.tab, bf16[1024,768]{1,0:T(8,128)(2,1)} %get-tuple-element.69.h2_ref, bf16[1024,3072]{1,0:T(8,128)(2,1)} %get-tuple-element.70.du_ref, ...), custom_call_target="tpu_custom_call" | custom-call | flops 12079595520 | bytes 31457280 | tf_op jit(solution)/shard_map/middle/pallas_call | solution.py:348
  281.3 18.8 %attend_back.2.da_ref.d_ref = bf16[3,1024,384]{2,1,0:T(8,128)(2,1)} custom-call(bf16[3,1024,384]{2,1,0:T(8,128)(2,1)} %get-tuple-element.61.q_ref.k_ref.v_ref, bf16[3,1024,384]{2,1,0:T(8,128)(2,1)} %get-tuple-element.61.q_ref.k_ref.v_ref, bf16[3,1024,384]{2,1,0:T(8,128)(2,1)} %get-tuple-element.61.q_ref.k_ref.v_ref, ...), custom_call_target="tpu_custom_call" | custom-call | flops 16106127360 | bytes 6291456 | tf_op jit(solution)/shard_map/attend_back/pallas_call | solution.py:403
  300.1 18.6 %attend_back.3.db_ref.d_ref = bf16[3,1024,384]{2,1,0:T(8,128)(2,1)} custom-call(bf16[3,1024,384]{2,1,0:T(8,128)(2,1)} %qkv_next.1.q_ref.k_ref.v_ref, bf16[3,1024,384]{2,1,0:T(8,128)(2,1)} %qkv_next.1.q_ref.k_ref.v_ref, bf16[3,1024,384]{2,1,0:T(8,128)(2,1)} %qkv_next.1.q_ref.k_ref.v_ref, bf16[1024,768]{1,0:T(8,128)(2,1)} %get-tuple-element.71.do_ref, ...), custom_call_target="tpu_custom_call" | custom-call | flops 16106127360 | bytes 6291456 | tf_op jit(solution)/shard_map/attend_back/pallas_call | solution.py:403
  318.7 6.6 %qkv_weight.3 = (bf16[8,48,1152]{2,1,0:T(8,128)(2,1)}, bf16[8,48,1152]{2,1,0:T(8,128)(2,1)}, f32[3,1,384]{2,1,0:T(1,128)}) custom-call(s32[9]{0:T(128)} %stack.114.tab, bf16[1024,768]{1,0:T(8,128)(2,1)} %get-tuple-element.63.x_ref.h_ref, bf16[3,1024,384]{2,1,0:T(8,128)(2,1)} %attend_back.3.db_ref.d_ref), custom_call_target="tpu_custom_call" | custom-call | flops 1811939328 | bytes 4718592 | tf_op jit(solution)/shard_map/qkv_weight/pallas_call | solution.py:435
  325.5 6.9 %qkv_weight.2 = (bf16[8,48,1152]{2,1,0:T(8,128)(2,1)}, bf16[8,48,1152]{2,1,0:T(8,128)(2,1)}, f32[3,1,384]{2,1,0:T(1,128)}) custom-call(s32[9]{0:T(128)} %stack.114.tab, bf16[1024,768]{1,0:T(8,128)(2,1)} %get-tuple-element.63.x_ref.h_ref, bf16[3,1024,384]{2,1,0:T(8,128)(2,1)} %attend_back.2.da_ref.d_ref), custom_call_target="tpu_custom_call" | custom-call | flops 1811939328 | bytes 4718592 | tf_op jit(solution)/shard_map/qkv_weight/pallas_call | solution.py:435
  332.8 11.7 %input_grad.1 = (f32[1024,768]{1,0:T(8,128)}, f32[8,768]{1,0:T(8,128)}) custom-call(s32[9]{0:T(128)} %stack.114.tab, bf16[3,1024,384]{2,1,0:T(8,128)(2,1)} %attend_back.2.da_ref.d_ref, bf16[3,1024,384]{2,1,0:T(8,128)(2,1)} %attend_back.3.db_ref.d_ref, bf16[1024,768]{1,0:T(8,128)(2,1)} %x_ref.5, f32[1024,768]{1,0:T(8,128)} %get-tuple-element.74.dx_ref, ...), custom_call_target="tpu_custom_call" | custom-call | flops 3623878656 | bytes 15728640 | tf_op jit(solution)/shard_map/input_grad/pallas_call | solution.py:482
  346.4 0.9 copy-done.6
  347.3 3.5 add_core.5
  350.8 1.4 collective-permute-start.27
  352.2 0.9 copy-done.5
  353.2 3.5 add_core.4
  357.6 15.1 %collective-permute-done.21.b = bf16[4,48,1152]{2,1,0:T(8,128)(2,1)S(1)} collective-permute-done((bf16[4,48,1152]{2,1,0:T(8,128)(2,1)}, bf16[4,48,1152]{2,1,0:T(8,128)(2,1)S(1)}, u32[]{:S(2)}, u32[]{:S(2)}) %collective-permute-start.21) | collective-permute-done | bytes 442400 | tf_op jit(solution)/shard_map/ppermute | solution.py:560
  372.7 1.0 copy-done.3
  373.9 5.2 %collective-permute-start.23 = (bf16[48,1152]{1,0:T(8,128)(2,1)S(1)}, bf16[48,1152]{1,0:T(8,128)(2,1)S(1)}, u32[]{:S(2)}, u32[]{:S(2)}) collective-permute-start(bf16[48,1152]{1,0:T(8,128)(2,1)S(1)} %get-tuple-element.82), channel_id=1, source_target_pairs={{0,16},{8,24},{16,0},{24,8},{1,17},{9,25},{17,1},{25,9},{2,18},{10... | collective-permute-start | bytes 331784 | tf_op jit(solution)/shard_map/ppermute | solution.py:560
  380.5 6.1 %all-to-all-start.1 = ((f32[32,1,576]{2,1,0:T(1,128)}), f32[32,1,576]{2,1,0:T(1,128)S(1)}, u32[]{:S(2)}, u32[]{:S(2)}) async-start(f32[32,1,576]{2,1,0:T(1,128)} %all_to_all.11), calls=%async_computation.1 | async-start | bytes 163840 | tf_op jit(solution)/shard_map/all_to_all | solution.py:679
  386.7 1.6 collective-permute-start.28
  388.3 1.9 collective-permute-start.29
  390.3 1.3 collective-permute-start.30
  391.7 1.7 collective-permute-start.25
  393.4 4.4 add_core.7
  399.0 1.2 collective-permute-done.30.d
  400.3 1.6 collective-permute-start.31
  401.8 5.0 add_core.6
  406.8 1.5 collective-permute-start.33
  408.4 18.4 %collective-permute-done.39.b = bf16[4,192,768]{2,1,0:T(8,128)(2,1)S(1)} collective-permute-done((bf16[4,192,768]{2,1,0:T(8,128)(2,1)}, bf16[4,192,768]{2,1,0:T(8,128)(2,1)S(1)}, u32[]{:S(2)}, u32[]{:S(2)}) %collective-permute-start.39) | collective-permute-done | bytes 1179680 | tf_op jit(solution)/shard_map/ppermute | solution.py:560
  427.1 1.1 collective-permute-start.40
  428.1 1.0 collective-permute-start.41
  429.2 1.5 collective-permute-start.42
  430.6 24.4 %collective-permute-done.33.b = bf16[4,48,3840]{2,1,0:T(8,128)(2,1)S(1)} collective-permute-done((bf16[4,48,3840]{2,1,0:T(8,128)(2,1)}, bf16[4,48,3840]{2,1,0:T(8,128)(2,1)S(1)}, u32[]{:S(2)}, u32[]{:S(2)}) %collective-permute-start.33) | collective-permute-done | bytes 1474592 | tf_op jit(solution)/shard_map/ppermute | solution.py:560
  455.3 2.5 collective-permute-start.34
  457.9 1.5 collective-permute-start.36
  460.2 11.2 %collective-permute-done.34.b = bf16[48,3840]{1,0:T(8,128)(2,1)S(1)} collective-permute-done((bf16[48,3840]{1,0:T(8,128)(2,1)S(1)}, bf16[48,3840]{1,0:T(8,128)(2,1)S(1)}, u32[]{:S(2)}, u32[]{:S(2)}) %collective-permute-start.34) | collective-permute-done | bytes 368672 | tf_op jit(solution)/shard_map/ppermute | solution.py:560
  471.3 11.3 %collective-permute-done.35.c = bf16[48,3840]{1,0:T(8,128)(2,1)S(1)} collective-permute-done((bf16[48,3840]{1,0:T(8,128)(2,1)S(1)}, bf16[48,3840]{1,0:T(8,128)(2,1)S(1)}, u32[]{:S(2)}, u32[]{:S(2)}) %collective-permute-start.35) | collective-permute-done | bytes 368672 | tf_op jit(solution)/shard_map/ppermute | solution.py:560
  482.6 7.1 %collective-permute-done.36.d = bf16[48,3840]{1,0:T(8,128)(2,1)S(1)} collective-permute-done((bf16[48,3840]{1,0:T(8,128)(2,1)S(1)}, bf16[48,3840]{1,0:T(8,128)(2,1)S(1)}, u32[]{:S(2)}, u32[]{:S(2)}) %collective-permute-start.36) | collective-permute-done | bytes 368672 | tf_op jit(solution)/shard_map/ppermute | solution.py:560
  492.2 5.8 %collective-permute-done.37 = bf16[48,3840]{1,0:T(8,128)(2,1)S(1)} collective-permute-done((bf16[48,3840]{1,0:T(8,128)(2,1)S(1)}, bf16[48,3840]{1,0:T(8,128)(2,1)S(1)}, u32[]{:S(2)}, u32[]{:S(2)}) %collective-permute-start.37) | collective-permute-done | bytes 368672 | tf_op jit(solution)/shard_map/ppermute | solution.py:560
  498.2 0.9 copy.18
  (181 shorter events, 29.6 us)
Async XLA Ops:
  0.6 18.2 %copy-start.7 = (bf16[147456]{0:T(1024)(128)(2,1)S(1)}, bf16[147456]{0:T(1024)(128)(2,1)}, u32[]{:S(2)}) copy-start(bf16[147456]{0:T(1024)(128)(2,1)} %param.12) | copy-start | bytes 884740
  0.6 19.1 %copy-start.4 = (bf16[147456]{0:T(1024)(128)(2,1)S(1)}, bf16[147456]{0:T(1024)(128)(2,1)}, u32[]{:S(2)}) copy-start(bf16[147456]{0:T(1024)(128)(2,1)} %param.13) | copy-start | bytes 884740
  2.0 20.8 %collective-permute-start = (bf16[48,1152]{1,0:T(8,128)(2,1)S(1)}, bf16[48,1152]{1,0:T(8,128)(2,1)S(1)}, u32[]{:S(2)}, u32[]{:S(2)}) collective-permute-start(bf16[48,1152]{1,0:T(8,128)(2,1)S(1)} %get-tuple-element.132), channel_id=1, source_target_pairs={{0,8},{8,0},{16,24},{24,16},{1,9},{9,1},{17,25},{25,17},{2,10},{10... | collective-permute-start | bytes 331784 | tf_op jit(solution)/shard_map/ppermute | solution.py:560
  3.6 20.9 %collective-permute-start.1 = (bf16[48,1152]{1,0:T(8,128)(2,1)S(1)}, bf16[48,1152]{1,0:T(8,128)(2,1)S(1)}, u32[]{:S(2)}, u32[]{:S(2)}) collective-permute-start(bf16[48,1152]{1,0:T(8,128)(2,1)S(1)} %get-tuple-element.132), channel_id=1, source_target_pairs={{0,16},{8,24},{16,0},{24,8},{1,17},{9,25},{17,1},{25,9},{2,18},{10... | collective-permute-start | bytes 331784 | tf_op jit(solution)/shard_map/ppermute | solution.py:560
  4.0 23.8 %collective-permute-start.2 = (bf16[48,1152]{1,0:T(8,128)(2,1)S(1)}, bf16[48,1152]{1,0:T(8,128)(2,1)S(1)}, u32[]{:S(2)}, u32[]{:S(2)}) collective-permute-start(bf16[48,1152]{1,0:T(8,128)(2,1)S(1)} %get-tuple-element.132), channel_id=1, source_target_pairs={{0,24},{8,16},{16,8},{24,0},{1,25},{9,17},{17,9},{25,1},{2,26},{10... | collective-permute-start | bytes 331784 | tf_op jit(solution)/shard_map/ppermute | solution.py:560
  5.6 23.2 %collective-permute-start.5 = (bf16[48,1152]{1,0:T(8,128)(2,1)S(1)}, bf16[48,1152]{1,0:T(8,128)(2,1)S(1)}, u32[]{:S(2)}, u32[]{:S(2)}) collective-permute-start(bf16[48,1152]{1,0:T(8,128)(2,1)S(1)} %get-tuple-element.130), channel_id=1, source_target_pairs={{0,8},{8,0},{16,24},{24,16},{1,9},{9,1},{17,25},{25,17},{2,10},{10... | collective-permute-start | bytes 331784 | tf_op jit(solution)/shard_map/ppermute | solution.py:560
  8.1 22.7 %collective-permute-start.6 = (bf16[48,1152]{1,0:T(8,128)(2,1)S(1)}, bf16[48,1152]{1,0:T(8,128)(2,1)S(1)}, u32[]{:S(2)}, u32[]{:S(2)}) collective-permute-start(bf16[48,1152]{1,0:T(8,128)(2,1)S(1)} %get-tuple-element.130), channel_id=1, source_target_pairs={{0,16},{8,24},{16,0},{24,8},{1,17},{9,25},{17,1},{25,9},{2,18},{10... | collective-permute-start | bytes 331784 | tf_op jit(solution)/shard_map/ppermute | solution.py:560
  10.9 10.9 %all-to-all-start = ((bf16[16,2,288]{2,1,0:T(2,128)(2,1)}), bf16[16,2,288]{2,1,0:T(2,128)(2,1)S(1)}, u32[]{:S(2)}, u32[]{:S(2)}) async-start(bf16[16,2,288]{2,1,0:T(2,128)(2,1)} %reshape.134), calls=%async_computation | async-start | bytes 49152 | tf_op jit(solution)/shard_map/all_to_all | solution.py:617
  22.8 8.6 %collective-permute-start.7 = (bf16[48,1152]{1,0:T(8,128)(2,1)S(1)}, bf16[48,1152]{1,0:T(8,128)(2,1)S(1)}, u32[]{:S(2)}, u32[]{:S(2)}) collective-permute-start(bf16[48,1152]{1,0:T(8,128)(2,1)S(1)} %get-tuple-element.130), channel_id=1, source_target_pairs={{0,24},{8,16},{16,8},{24,0},{1,25},{9,17},{17,9},{25,1},{2,26},{10... | collective-permute-start | bytes 331784 | tf_op jit(solution)/shard_map/ppermute | solution.py:560
  24.6 57.6 %collective-permute-start.10 = (bf16[48,3840]{1,0:T(8,128)(2,1)S(1)}, bf16[48,3840]{1,0:T(8,128)(2,1)S(1)}, u32[]{:S(2)}, u32[]{:S(2)}) collective-permute-start(bf16[48,3840]{1,0:T(8,128)(2,1)S(1)} %constant_dynamic-update-slice_fusion.10), channel_id=1, source_target_pairs={{0,8},{8,0},{16,24},{24,16},{1,9},{9,1},{17,25},{25,17},{2,10},{10... | collective-permute-start | bytes 1105928 | tf_op jit(solution)/shard_map/ppermute | solution.py:560
  27.8 55.0 %collective-permute-start.11 = (bf16[48,3840]{1,0:T(8,128)(2,1)S(1)}, bf16[48,3840]{1,0:T(8,128)(2,1)S(1)}, u32[]{:S(2)}, u32[]{:S(2)}) collective-permute-start(bf16[48,3840]{1,0:T(8,128)(2,1)S(1)} %constant_dynamic-update-slice_fusion.10), channel_id=1, source_target_pairs={{0,16},{8,24},{16,0},{24,8},{1,17},{9,25},{17,1},{25,9},{2,18},{10... | collective-permute-start | bytes 1105928 | tf_op jit(solution)/shard_map/ppermute | solution.py:560
  28.7 28.4 %collective-permute-start.15 = (bf16[192,768]{1,0:T(8,128)(2,1)S(1)}, bf16[192,768]{1,0:T(8,128)(2,1)S(1)}, u32[]{:S(2)}, u32[]{:S(2)}) collective-permute-start(bf16[192,768]{1,0:T(8,128)(2,1)S(1)} %reshape.106), channel_id=1, source_target_pairs={{0,8},{8,0},{16,24},{24,16},{1,9},{9,1},{17,25},{25,17},{2,10},{10... | collective-permute-start | bytes 884744 | tf_op jit(solution)/shard_map/ppermute | solution.py:560
  30.8 41.2 %collective-permute-start.16 = (bf16[192,768]{1,0:T(8,128)(2,1)S(1)}, bf16[192,768]{1,0:T(8,128)(2,1)S(1)}, u32[]{:S(2)}, u32[]{:S(2)}) collective-permute-start(bf16[192,768]{1,0:T(8,128)(2,1)S(1)} %reshape.106), channel_id=1, source_target_pairs={{0,16},{8,24},{16,0},{24,8},{1,17},{9,25},{17,1},{25,9},{2,18},{10... | collective-permute-start | bytes 884744 | tf_op jit(solution)/shard_map/ppermute | solution.py:560
  31.5 48.3 %collective-permute-start.17 = (bf16[192,768]{1,0:T(8,128)(2,1)S(1)}, bf16[192,768]{1,0:T(8,128)(2,1)S(1)}, u32[]{:S(2)}, u32[]{:S(2)}) collective-permute-start(bf16[192,768]{1,0:T(8,128)(2,1)S(1)} %reshape.106), channel_id=1, source_target_pairs={{0,24},{8,16},{16,8},{24,0},{1,25},{9,17},{17,9},{25,1},{2,26},{10... | collective-permute-start | bytes 884744 | tf_op jit(solution)/shard_map/ppermute | solution.py:560
  57.1 30.2 %collective-permute-start.12 = (bf16[48,3840]{1,0:T(8,128)(2,1)S(1)}, bf16[48,3840]{1,0:T(8,128)(2,1)S(1)}, u32[]{:S(2)}, u32[]{:S(2)}) collective-permute-start(bf16[48,3840]{1,0:T(8,128)(2,1)S(1)} %constant_dynamic-update-slice_fusion.10), channel_id=1, source_target_pairs={{0,24},{8,16},{16,8},{24,0},{1,25},{9,17},{17,9},{25,1},{2,26},{10... | collective-permute-start | bytes 1105928 | tf_op jit(solution)/shard_map/ppermute | solution.py:560
  71.9 77.1 %collective-permute-start.3 = (bf16[4,48,1152]{2,1,0:T(8,128)(2,1)S(1)}, bf16[4,48,1152]{2,1,0:T(8,128)(2,1)S(1)}, u32[]{:S(2)}, u32[]{:S(2)}) collective-permute-start(bf16[4,48,1152]{2,1,0:T(8,128)(2,1)S(1)} %pad_maximum_fusion.2), channel_id=1, source_target_pairs={{0,4},{4,0},{1,5},{5,1},{2,6},{6,2},{3,7},{7,3},{8,12},{12,8},{9,1... | collective-permute-start | bytes 1327112 | tf_op jit(solution)/shard_map/ppermute | solution.py:560
  79.8 69.8 %collective-permute-start.8 = (bf16[4,48,1152]{2,1,0:T(8,128)(2,1)S(1)}, bf16[4,48,1152]{2,1,0:T(8,128)(2,1)S(1)}, u32[]{:S(2)}, u32[]{:S(2)}) collective-permute-start(bf16[4,48,1152]{2,1,0:T(8,128)(2,1)S(1)} %pad_maximum_fusion.3), channel_id=1, source_target_pairs={{0,4},{4,0},{1,5},{5,1},{2,6},{6,2},{3,7},{7,3},{8,12},{12,8},{9,1... | collective-permute-start | bytes 1327112 | tf_op jit(solution)/shard_map/ppermute | solution.py:560
  81.4 7.6 %copy-start.8 = (bf16[8,48,3840]{2,1,0:T(8,128)(2,1)S(1)}, bf16[8,48,3840]{2,1,0:T(8,128)(2,1)}, u32[]{:S(2)}) copy-start(bf16[8,48,3840]{2,1,0:T(8,128)(2,1)} %constant_dynamic-update-slice_fusion.16) | copy-start | bytes 8847364
  82.2 68.4 %collective-permute-start.18 = (bf16[4,192,768]{2,1,0:T(8,128)(2,1)S(1)}, bf16[4,192,768]{2,1,0:T(8,128)(2,1)S(1)}, u32[]{:S(2)}, u32[]{:S(2)}) collective-permute-start(bf16[4,192,768]{2,1,0:T(8,128)(2,1)S(1)} %pad_maximum_fusion.1), channel_id=1, source_target_pairs={{0,4},{4,0},{1,5},{5,1},{2,6},{6,2},{3,7},{7,3},{8,12},{12,8},{9,1... | collective-permute-start | bytes 3538952 | tf_op jit(solution)/shard_map/ppermute | solution.py:560
  87.5 60.6 %collective-permute-start.13 = (bf16[4,48,3840]{2,1,0:T(8,128)(2,1)S(1)}, bf16[4,48,3840]{2,1,0:T(8,128)(2,1)S(1)}, u32[]{:S(2)}, u32[]{:S(2)}) collective-permute-start(bf16[4,48,3840]{2,1,0:T(8,128)(2,1)S(1)} %pad_maximum_fusion), channel_id=1, source_target_pairs={{0,4},{4,0},{1,5},{5,1},{2,6},{6,2},{3,7},{7,3},{8,12},{12,8},{9,1... | collective-permute-start | bytes 4423688 | tf_op jit(solution)/shard_map/ppermute | solution.py:560
  89.0 60.0 %copy-start.11 = (bf16[8,48,1152]{2,1,0:T(8,128)(2,1)S(1)}, bf16[8,48,1152]{2,1,0:T(8,128)(2,1)}, u32[]{:S(2)}) copy-start(bf16[8,48,1152]{2,1,0:T(8,128)(2,1)} %constant_dynamic-update-slice_fusion.1) | copy-start | bytes 2654212
  148.1 3.6 copy-start.9
  148.1 54.5 %collective-permute-start.14 = (bf16[8,48,3840]{2,1,0:T(8,128)(2,1)S(1)}, bf16[8,48,3840]{2,1,0:T(8,128)(2,1)}, u32[]{:S(2)}, u32[]{:S(2)}) collective-permute-start(bf16[8,48,3840]{2,1,0:T(8,128)(2,1)S(1)} %constant_dynamic-update-slice_fusion.12.mine), channel_id=1, source_target_pairs={{0,2},{2,0},{1,3},{3,1},{4,6},{6,4},{5,7},{7,5},{8,10},{10,8},{9,1... | collective-permute-start | bytes 8847368 | tf_op jit(solution)/shard_map/ppermute | solution.py:560
  149.1 5.7 %copy-start.12 = (bf16[8,48,1152]{2,1,0:T(8,128)(2,1)}, bf16[8,48,1152]{2,1,0:T(8,128)(2,1)S(1)}, u32[]{:S(2)}) copy-start(bf16[8,48,1152]{2,1,0:T(8,128)(2,1)S(1)} %constant_dynamic-update-slice_fusion.mine.ma) | copy-start | bytes 2654212
  149.1 5.7 %collective-permute-start.4 = (bf16[8,48,1152]{2,1,0:T(8,128)(2,1)S(1)}, bf16[8,48,1152]{2,1,0:T(8,128)(2,1)S(1)}, u32[]{:S(2)}, u32[]{:S(2)}) collective-permute-start(bf16[8,48,1152]{2,1,0:T(8,128)(2,1)S(1)} %constant_dynamic-update-slice_fusion.mine.ma), channel_id=1, source_target_pairs={{0,2},{2,0},{1,3},{3,1},{4,6},{6,4},{5,7},{7,5},{8,10},{10,8},{9,1... | collective-permute-start | bytes 2654216 | tf_op jit(solution)/shard_map/ppermute | solution.py:560
  149.6 14.0 %copy-start.10 = (bf16[8,48,1152]{2,1,0:T(8,128)(2,1)}, bf16[8,48,1152]{2,1,0:T(8,128)(2,1)S(1)}, u32[]{:S(2)}) copy-start(bf16[8,48,1152]{2,1,0:T(8,128)(2,1)S(1)} %constant_dynamic-update-slice_fusion.5.mine.mb) | copy-start | bytes 2654212
  149.6 14.0 %collective-permute-start.9 = (bf16[8,48,1152]{2,1,0:T(8,128)(2,1)S(1)}, bf16[8,48,1152]{2,1,0:T(8,128)(2,1)S(1)}, u32[]{:S(2)}, u32[]{:S(2)}) collective-permute-start(bf16[8,48,1152]{2,1,0:T(8,128)(2,1)S(1)} %constant_dynamic-update-slice_fusion.5.mine.mb), channel_id=1, source_target_pairs={{0,2},{2,0},{1,3},{3,1},{4,6},{6,4},{5,7},{7,5},{8,10},{10,8},{9,1... | collective-permute-start | bytes 2654216 | tf_op jit(solution)/shard_map/ppermute | solution.py:560
  151.7 80.8 %collective-permute-start.19 = (bf16[8,192,768]{2,1,0:T(8,128)(2,1)}, bf16[8,192,768]{2,1,0:T(8,128)(2,1)}, u32[]{:S(2)}, u32[]{:S(2)}) collective-permute-start(bf16[8,192,768]{2,1,0:T(8,128)(2,1)} %constant_dynamic-update-slice_fusion.17), channel_id=1, source_target_pairs={{0,2},{2,0},{1,3},{3,1},{4,6},{6,4},{5,7},{7,5},{8,10},{10,8},{9,1... | collective-permute-start | bytes 7077896 | tf_op jit(solution)/shard_map/ppermute | solution.py:560
  163.6 0.9 copy-start.18
  256.6 135.0 %collective-permute-start.38 = (bf16[8,192,768]{2,1,0:T(8,128)(2,1)}, bf16[8,192,768]{2,1,0:T(8,128)(2,1)}, u32[]{:S(2)}, u32[]{:S(2)}) collective-permute-start(bf16[8,192,768]{2,1,0:T(8,128)(2,1)} %bitcast.90), channel_id=1, source_target_pairs={{0,2},{2,0},{1,3},{3,1},{4,6},{6,4},{5,7},{7,5},{8,10},{10,8},{9,1... | collective-permute-start | bytes 7077896 | tf_op jit(solution)/shard_map/ppermute | solution.py:560
  280.8 121.0 %collective-permute-start.32 = (bf16[8,48,3840]{2,1,0:T(8,128)(2,1)}, bf16[8,48,3840]{2,1,0:T(8,128)(2,1)}, u32[]{:S(2)}, u32[]{:S(2)}) collective-permute-start(bf16[8,48,3840]{2,1,0:T(8,128)(2,1)} %get-tuple-element.93), channel_id=1, source_target_pairs={{0,2},{2,0},{1,3},{3,1},{4,6},{6,4},{5,7},{7,5},{8,10},{10,8},{9,1... | collective-permute-start | bytes 8847368 | tf_op jit(solution)/shard_map/ppermute | solution.py:560
  325.4 7.4 %copy-start.14 = (f32[1,768]{1,0:T(1,128)S(1)}, f32[1,768]{1,0:T(1,128)}, u32[]{:S(2)}) copy-start(f32[1,768]{1,0:T(1,128)} %get-tuple-element.113) | copy-start | bytes 9220
  325.4 21.0 %collective-permute-start.26 = (bf16[8,48,1152]{2,1,0:T(8,128)(2,1)}, bf16[8,48,1152]{2,1,0:T(8,128)(2,1)S(1)}, u32[]{:S(2)}, u32[]{:S(2)}) collective-permute-start(bf16[8,48,1152]{2,1,0:T(8,128)(2,1)} %get-tuple-element.85), channel_id=1, source_target_pairs={{0,2},{2,0},{1,3},{3,1},{4,6},{6,4},{5,7},{7,5},{8,10},{10,8},{9,1... | collective-permute-start | bytes 2654216 | tf_op jit(solution)/shard_map/ppermute | solution.py:560
  332.4 19.8 %collective-permute-start.20 = (bf16[8,48,1152]{2,1,0:T(8,128)(2,1)}, bf16[8,48,1152]{2,1,0:T(8,128)(2,1)S(1)}, u32[]{:S(2)}, u32[]{:S(2)}) collective-permute-start(bf16[8,48,1152]{2,1,0:T(8,128)(2,1)} %get-tuple-element.77), channel_id=1, source_target_pairs={{0,2},{2,0},{1,3},{3,1},{4,6},{6,4},{5,7},{7,5},{8,10},{10,8},{9,1... | collective-permute-start | bytes 2654216 | tf_op jit(solution)/shard_map/ppermute | solution.py:560
  332.8 12.5 %copy-start.16 = (f32[3,1,384]{2,1,0:T(1,128)S(1)}, f32[3,1,384]{2,1,0:T(1,128)}, u32[]{:S(2)}) copy-start(f32[3,1,384]{2,1,0:T(1,128)} %get-tuple-element.110) | copy-start | bytes 13828
  332.8 12.6 %copy-start.15 = (f32[3,1,384]{2,1,0:T(1,128)S(1)}, f32[3,1,384]{2,1,0:T(1,128)}, u32[]{:S(2)}) copy-start(f32[3,1,384]{2,1,0:T(1,128)} %get-tuple-element.111) | copy-start | bytes 13828
  344.5 12.8 %copy-start.13 = (f32[1,3072]{1,0:T(1,128)S(1)}, f32[1,3072]{1,0:T(1,128)}, u32[]{:S(2)}) copy-start(f32[1,3072]{1,0:T(1,128)} %get-tuple-element.112) | copy-start | bytes 36868
  346.3 0.9 copy-start.6
  350.8 35.8 %copy-start.2 = (bf16[4,48,1152]{2,1,0:T(8,128)(2,1)S(1)}, bf16[4,48,1152]{2,1,0:T(8,128)(2,1)}, u32[]{:S(2)}) copy-start(bf16[4,48,1152]{2,1,0:T(8,128)(2,1)} %get-tuple-element.86.a) | copy-start | bytes 1327108
  350.8 28.3 %collective-permute-start.27 = (bf16[4,48,1152]{2,1,0:T(8,128)(2,1)}, bf16[4,48,1152]{2,1,0:T(8,128)(2,1)S(1)}, u32[]{:S(2)}, u32[]{:S(2)}) collective-permute-start(bf16[4,48,1152]{2,1,0:T(8,128)(2,1)} %get-tuple-element.87), channel_id=1, source_target_pairs={{0,4},{4,0},{1,5},{5,1},{2,6},{6,2},{3,7},{7,3},{8,12},{12,8},{9,1... | collective-permute-start | bytes 1327112 | tf_op jit(solution)/shard_map/ppermute | solution.py:560
  352.2 0.9 copy-start.5
  356.7 16.0 %collective-permute-start.21 = (bf16[4,48,1152]{2,1,0:T(8,128)(2,1)}, bf16[4,48,1152]{2,1,0:T(8,128)(2,1)S(1)}, u32[]{:S(2)}, u32[]{:S(2)}) collective-permute-start(bf16[4,48,1152]{2,1,0:T(8,128)(2,1)} %get-tuple-element.79), channel_id=1, source_target_pairs={{0,4},{4,0},{1,5},{5,1},{2,6},{6,2},{3,7},{7,3},{8,12},{12,8},{9,1... | collective-permute-start | bytes 1327112 | tf_op jit(solution)/shard_map/ppermute | solution.py:560
  372.7 1.0 copy-start.3
  373.8 12.9 %collective-permute-start.22 = (bf16[48,1152]{1,0:T(8,128)(2,1)S(1)}, bf16[48,1152]{1,0:T(8,128)(2,1)S(1)}, u32[]{:S(2)}, u32[]{:S(2)}) collective-permute-start(bf16[48,1152]{1,0:T(8,128)(2,1)S(1)} %get-tuple-element.81), channel_id=1, source_target_pairs={{0,8},{8,0},{16,24},{24,16},{1,9},{9,1},{17,25},{25,17},{2,10},{10... | collective-permute-start | bytes 331784 | tf_op jit(solution)/shard_map/ppermute | solution.py:560
  373.9 14.5 %collective-permute-start.23 = (bf16[48,1152]{1,0:T(8,128)(2,1)S(1)}, bf16[48,1152]{1,0:T(8,128)(2,1)S(1)}, u32[]{:S(2)}, u32[]{:S(2)}) collective-permute-start(bf16[48,1152]{1,0:T(8,128)(2,1)S(1)} %get-tuple-element.82), channel_id=1, source_target_pairs={{0,16},{8,24},{16,0},{24,8},{1,17},{9,25},{17,1},{25,9},{2,18},{10... | collective-permute-start | bytes 331784 | tf_op jit(solution)/shard_map/ppermute | solution.py:560
  379.1 11.1 %collective-permute-start.24 = (bf16[48,1152]{1,0:T(8,128)(2,1)S(1)}, bf16[48,1152]{1,0:T(8,128)(2,1)S(1)}, u32[]{:S(2)}, u32[]{:S(2)}) collective-permute-start(bf16[48,1152]{1,0:T(8,128)(2,1)S(1)} %get-tuple-element.83), channel_id=1, source_target_pairs={{0,24},{8,16},{16,8},{24,0},{1,25},{9,17},{17,9},{25,1},{2,26},{10... | collective-permute-start | bytes 331784 | tf_op jit(solution)/shard_map/ppermute | solution.py:560
  380.5 17.3 %all-to-all-start.1 = ((f32[32,1,576]{2,1,0:T(1,128)}), f32[32,1,576]{2,1,0:T(1,128)S(1)}, u32[]{:S(2)}, u32[]{:S(2)}) async-start(f32[32,1,576]{2,1,0:T(1,128)} %all_to_all.11), calls=%async_computation.1 | async-start | bytes 163840 | tf_op jit(solution)/shard_map/all_to_all | solution.py:679
  386.7 11.0 %collective-permute-start.28 = (bf16[48,1152]{1,0:T(8,128)(2,1)S(1)}, bf16[48,1152]{1,0:T(8,128)(2,1)S(1)}, u32[]{:S(2)}, u32[]{:S(2)}) collective-permute-start(bf16[48,1152]{1,0:T(8,128)(2,1)S(1)} %get-tuple-element.89), channel_id=1, source_target_pairs={{0,8},{8,0},{16,24},{24,16},{1,9},{9,1},{17,25},{25,17},{2,10},{10... | collective-permute-start | bytes 331784 | tf_op jit(solution)/shard_map/ppermute | solution.py:560
  388.3 10.7 %collective-permute-start.29 = (bf16[48,1152]{1,0:T(8,128)(2,1)S(1)}, bf16[48,1152]{1,0:T(8,128)(2,1)S(1)}, u32[]{:S(2)}, u32[]{:S(2)}) collective-permute-start(bf16[48,1152]{1,0:T(8,128)(2,1)S(1)} %get-tuple-element.90), channel_id=1, source_target_pairs={{0,16},{8,24},{16,0},{24,8},{1,17},{9,25},{17,1},{25,9},{2,18},{10... | collective-permute-start | bytes 331784 | tf_op jit(solution)/shard_map/ppermute | solution.py:560
  390.3 9.9 %collective-permute-start.30 = (bf16[48,1152]{1,0:T(8,128)(2,1)S(1)}, bf16[48,1152]{1,0:T(8,128)(2,1)S(1)}, u32[]{:S(2)}, u32[]{:S(2)}) collective-permute-start(bf16[48,1152]{1,0:T(8,128)(2,1)S(1)} %get-tuple-element.91), channel_id=1, source_target_pairs={{0,24},{8,16},{16,8},{24,0},{1,25},{9,17},{17,9},{25,1},{2,26},{10... | collective-permute-start | bytes 331784 | tf_op jit(solution)/shard_map/ppermute | solution.py:560
  391.7 16.6 %collective-permute-start.25 = (bf16[48,1152]{1,0:T(8,128)(2,1)S(1)}, bf16[48,1152]{1,0:T(8,128)(2,1)S(1)}, u32[]{:S(2)}, u32[]{:S(2)}) collective-permute-start(bf16[48,1152]{1,0:T(8,128)(2,1)S(1)} %add_z.4), channel_id=1, source_target_pairs={{0,1},{1,0},{2,3},{3,2},{4,5},{5,4},{6,7},{7,6},{8,9},{9,8},{10,11... | collective-permute-start | bytes 331784 | tf_op jit(solution)/shard_map/ppermute | solution.py:560
  397.8 29.1 %collective-permute-start.39 = (bf16[4,192,768]{2,1,0:T(8,128)(2,1)}, bf16[4,192,768]{2,1,0:T(8,128)(2,1)S(1)}, u32[]{:S(2)}, u32[]{:S(2)}) collective-permute-start(bf16[4,192,768]{2,1,0:T(8,128)(2,1)} %get-tuple-element.103), channel_id=1, source_target_pairs={{0,4},{4,0},{1,5},{5,1},{2,6},{6,2},{3,7},{7,3},{8,12},{12,8},{9,1... | collective-permute-start | bytes 3538952 | tf_op jit(solution)/shard_map/ppermute | solution.py:560
  400.3 8.1 %collective-permute-start.31 = (bf16[48,1152]{1,0:T(8,128)(2,1)S(1)}, bf16[48,1152]{1,0:T(8,128)(2,1)S(1)}, u32[]{:S(2)}, u32[]{:S(2)}) collective-permute-start(bf16[48,1152]{1,0:T(8,128)(2,1)S(1)} %add_z.5), channel_id=1, source_target_pairs={{0,1},{1,0},{2,3},{3,2},{4,5},{5,4},{6,7},{7,6},{8,9},{9,8},{10,11... | collective-permute-start | bytes 331784 | tf_op jit(solution)/shard_map/ppermute | solution.py:560
  401.8 25.0 %copy-start.1 = (bf16[4,192,768]{2,1,0:T(8,128)(2,1)S(1)}, bf16[4,192,768]{2,1,0:T(8,128)(2,1)}, u32[]{:S(2)}) copy-start(bf16[4,192,768]{2,1,0:T(8,128)(2,1)} %get-tuple-element.102.a) | copy-start | bytes 3538948
  406.8 48.2 %copy-start = (bf16[4,48,3840]{2,1,0:T(8,128)(2,1)S(1)}, bf16[4,48,3840]{2,1,0:T(8,128)(2,1)}, u32[]{:S(2)}) copy-start(bf16[4,48,3840]{2,1,0:T(8,128)(2,1)} %get-tuple-element.94.a) | copy-start | bytes 4423684
  406.8 48.2 %collective-permute-start.33 = (bf16[4,48,3840]{2,1,0:T(8,128)(2,1)}, bf16[4,48,3840]{2,1,0:T(8,128)(2,1)S(1)}, u32[]{:S(2)}, u32[]{:S(2)}) collective-permute-start(bf16[4,48,3840]{2,1,0:T(8,128)(2,1)} %get-tuple-element.95), channel_id=1, source_target_pairs={{0,4},{4,0},{1,5},{5,1},{2,6},{6,2},{3,7},{7,3},{8,12},{12,8},{9,1... | collective-permute-start | bytes 4423688 | tf_op jit(solution)/shard_map/ppermute | solution.py:560
  427.1 30.8 %collective-permute-start.40 = (bf16[192,768]{1,0:T(8,128)(2,1)S(1)}, bf16[192,768]{1,0:T(8,128)(2,1)S(1)}, u32[]{:S(2)}, u32[]{:S(2)}) collective-permute-start(bf16[192,768]{1,0:T(8,128)(2,1)S(1)} %get-tuple-element.105), channel_id=1, source_target_pairs={{0,8},{8,0},{16,24},{24,16},{1,9},{9,1},{17,25},{25,17},{2,10},{10... | collective-permute-start | bytes 884744 | tf_op jit(solution)/shard_map/ppermute | solution.py:560
  428.1 31.2 %collective-permute-start.41 = (bf16[192,768]{1,0:T(8,128)(2,1)S(1)}, bf16[192,768]{1,0:T(8,128)(2,1)S(1)}, u32[]{:S(2)}, u32[]{:S(2)}) collective-permute-start(bf16[192,768]{1,0:T(8,128)(2,1)S(1)} %get-tuple-element.106), channel_id=1, source_target_pairs={{0,16},{8,24},{16,0},{24,8},{1,17},{9,25},{17,1},{25,9},{2,18},{10... | collective-permute-start | bytes 884744 | tf_op jit(solution)/shard_map/ppermute | solution.py:560
  429.2 30.2 %collective-permute-start.42 = (bf16[192,768]{1,0:T(8,128)(2,1)S(1)}, bf16[192,768]{1,0:T(8,128)(2,1)S(1)}, u32[]{:S(2)}, u32[]{:S(2)}) collective-permute-start(bf16[192,768]{1,0:T(8,128)(2,1)S(1)} %get-tuple-element.107), channel_id=1, source_target_pairs={{0,24},{8,16},{16,8},{24,0},{1,25},{9,17},{17,9},{25,1},{2,26},{10... | collective-permute-start | bytes 884744 | tf_op jit(solution)/shard_map/ppermute | solution.py:560
  455.3 16.0 %collective-permute-start.34 = (bf16[48,3840]{1,0:T(8,128)(2,1)S(1)}, bf16[48,3840]{1,0:T(8,128)(2,1)S(1)}, u32[]{:S(2)}, u32[]{:S(2)}) collective-permute-start(bf16[48,3840]{1,0:T(8,128)(2,1)S(1)} %get-tuple-element.97), channel_id=1, source_target_pairs={{0,8},{8,0},{16,24},{24,16},{1,9},{9,1},{17,25},{25,17},{2,10},{10... | collective-permute-start | bytes 1105928 | tf_op jit(solution)/shard_map/ppermute | solution.py:560
  457.8 24.8 %collective-permute-start.35 = (bf16[48,3840]{1,0:T(8,128)(2,1)S(1)}, bf16[48,3840]{1,0:T(8,128)(2,1)S(1)}, u32[]{:S(2)}, u32[]{:S(2)}) collective-permute-start(bf16[48,3840]{1,0:T(8,128)(2,1)S(1)} %get-tuple-element.98), channel_id=1, source_target_pairs={{0,16},{8,24},{16,0},{24,8},{1,17},{9,25},{17,1},{25,9},{2,18},{10... | collective-permute-start | bytes 1105928 | tf_op jit(solution)/shard_map/ppermute | solution.py:560
  457.9 31.9 %collective-permute-start.36 = (bf16[48,3840]{1,0:T(8,128)(2,1)S(1)}, bf16[48,3840]{1,0:T(8,128)(2,1)S(1)}, u32[]{:S(2)}, u32[]{:S(2)}) collective-permute-start(bf16[48,3840]{1,0:T(8,128)(2,1)S(1)} %get-tuple-element.99), channel_id=1, source_target_pairs={{0,24},{8,16},{16,8},{24,0},{1,25},{9,17},{17,9},{25,1},{2,26},{10... | collective-permute-start | bytes 1105928 | tf_op jit(solution)/shard_map/ppermute | solution.py:560
  459.6 31.8 %collective-permute-start.43 = (bf16[192,768]{1,0:T(8,128)(2,1)S(1)}, bf16[192,768]{1,0:T(8,128)(2,1)S(1)}, u32[]{:S(2)}, u32[]{:S(2)}) collective-permute-start(bf16[192,768]{1,0:T(8,128)(2,1)S(1)} %add_z.7), channel_id=1, source_target_pairs={{0,1},{1,0},{2,3},{3,2},{4,5},{5,4},{6,7},{7,6},{8,9},{9,8},{10,11... | collective-permute-start | bytes 884744 | tf_op jit(solution)/shard_map/ppermute | solution.py:560
  489.9 8.1 %collective-permute-start.37 = (bf16[48,3840]{1,0:T(8,128)(2,1)S(1)}, bf16[48,3840]{1,0:T(8,128)(2,1)S(1)}, u32[]{:S(2)}, u32[]{:S(2)}) collective-permute-start(bf16[48,3840]{1,0:T(8,128)(2,1)S(1)} %add_z.6), channel_id=1, source_target_pairs={{0,1},{1,0},{2,3},{3,2},{4,5},{5,4},{6,7},{7,6},{8,9},{9,8},{10,11... | collective-permute-start | bytes 1105928 | tf_op jit(solution)/shard_map/ppermute | solution.py:560
  (1 other events, 0.9 us)
